TPU v7x, 32 devices: a whole 2x2x4 slice. The times are simulated.
32 devices in a mesh: energy: 8 (over z, core), layer: 4 (over y, x).
Axes of the slice: x: 2, y: 2, z: 4, core: 2. Of those that a mesh axis runs over, the one named last changes fastest.
Arguments:
- green_blocks: bfloat16 [8, 12, 12, 1536], P('energy', None, None, 'layer'), as said below
- coupling: bfloat16 [12, 12, 4, 1536], P(None, None, None, 'layer'), may hold values from -1.75 to 1.75
- phonon_weights: float32 [2, 48, 4, 1536], P(None, None, None, 'layer'), may hold values from 0.001 to 0.01
- neighbours: int32 [4, 1536], P(None, 'layer'), may hold values from 0 to 1151, as said below
- phonon_shifts: int32 [48], replicated, may hold values from 1 to 2
Outputs:
- corrected: bfloat16 [8, 12, 12, 1536], P('energy', None, None, 'layer')
- polarization: float32 [48, 4, 1536], P(None, None, ('layer', 'energy'))
Inputs may be any that keep to these rules, and one draw needn't show every extreme that they name: Every 12 x 12 block green_blocks[E, :, :, a] is symmetric. neighbours[k, a] is a place in the window of atom a: places 0 to 383 are the previous layer block, then the own block, then the next one. Slot 0 lies in the previous block, slot 1 in the next block, the other slots in the own block and never name the atom itself.
All inputs are finite; a program needn't handle non-finite values.
Results may differ from a plain program's by a relative error of at most 0.0062.
Values may be sent and summed in bfloat16 or wider, within the bound.
A program may use at most 128 MiB of HBM per device.

v0:
```python
import math

import jax
import jax.numpy as jnp
import numpy as np
from jax import lax
from jax.sharding import PartitionSpec as P

NO = 12
NBR = 4


def with_halo(cells, sides, width):
    for axis, dim in sides:
        count = lax.axis_size(axis)
        ends = count - 1
        head = lax.slice_in_dim(cells, 0, width, axis=dim)
        tail = lax.slice_in_dim(cells, cells.shape[dim] - width, cells.shape[dim], axis=dim)
        cells = jnp.concatenate(
            [
                lax.ppermute(tail, axis, [(i, (i + 1) % count) for i in range(ends)]),
                cells,
                lax.ppermute(head, axis, [((i + 1) % count, i) for i in range(ends)]),
            ],
            axis=dim,
        )
    return cells


def triangle_tables(matrix_order):
    index_pairs = [
        (first_index, second_index)
        for first_index in range(matrix_order)
        for second_index in range(first_index, matrix_order)
    ]
    upper_picks = np.array(
        [first_index * matrix_order + second_index for first_index, second_index in index_pairs],
        dtype=np.int32,
    )
    lookup = np.zeros(matrix_order * matrix_order, dtype=np.int32)
    for position, (first_index, second_index) in enumerate(index_pairs):
        lookup[first_index * matrix_order + second_index] = position
        lookup[second_index * matrix_order + first_index] = position
    return (upper_picks, lookup)


def shift_tables(phonon_shifts, energy_count):
    energies = jnp.arange(energy_count, dtype=jnp.int32)
    target = energies[None, :, None]
    source = energies[None, None, :]
    offsets = phonon_shifts[:, None, None]
    lower_table = (source == target - offsets).astype(jnp.float32)
    upper_table = (source == target + offsets).astype(jnp.float32)
    return (lower_table, upper_table)


def body(green_blocks, coupling, phonon_weights, neighbours, phonon_shifts):
    highest = lax.Precision.HIGHEST
    energy_count = lax.axis_size("energy")
    local_energies = green_blocks.shape[0]
    slab_atoms = green_blocks.shape[3]
    owned_atoms = slab_atoms // energy_count
    energy_total = local_energies * energy_count
    entries = NO * NO
    upper_picks, lookup = triangle_tables(NO)
    window = with_halo(green_blocks, (("layer", 3),), slab_atoms)
    gathered = jnp.take(window, neighbours, axis=3)
    first_product = jnp.einsum(
        "ipka,epqka->eiqka", coupling, gathered, preferred_element_type=jnp.float32
    )
    product = jnp.einsum(
        "eiqka,jqka->eakij", first_product, coupling.astype(jnp.float32), precision=highest
    ).astype(jnp.bfloat16)
    product = product.reshape(local_energies, energy_count, owned_atoms, NBR, entries)
    own_green = jnp.transpose(
        green_blocks.reshape(local_energies, entries, energy_count, owned_atoms), (0, 2, 3, 1)
    )
    product_send = product[..., upper_picks]
    green_send = own_green[..., upper_picks]
    product_moved, green_moved = (
        lax.all_to_all(product_send, "energy", split_axis=1, concat_axis=0, tiled=True),
        lax.all_to_all(green_send, "energy", split_axis=1, concat_axis=0, tiled=True),
    )
    product_moved = product_moved[..., lookup]
    green_moved = green_moved[..., lookup]
    product_all = product_moved.reshape(energy_total, owned_atoms, NBR, entries)
    green_all = green_moved.reshape(energy_total, owned_atoms, entries)
    atom_start = lax.axis_index("energy") * owned_atoms
    owned_weights = lax.dynamic_slice_in_dim(phonon_weights, atom_start, owned_atoms, 3)
    lower_table, upper_table = shift_tables(phonon_shifts, energy_total)
    kernel = jnp.einsum("wka,wef->akef", owned_weights[0], lower_table, precision=highest)
    kernel = kernel + jnp.einsum("wka,wef->akef", owned_weights[1], upper_table, precision=highest)
    self_energy = jnp.einsum(
        "akef,fakc->eac", kernel, product_all.astype(jnp.float32), precision=highest
    ).astype(jnp.bfloat16)
    correlation = jnp.einsum(
        "fakc,eac->akfe", product_all, green_all, preferred_element_type=jnp.float32
    )
    norm_factor = 1.0 / (NO * math.sqrt(energy_total))
    polarization = (
        jnp.einsum("wef,akfe->wka", upper_table, correlation, precision=highest) * norm_factor
    )
    self_send = self_energy[..., upper_picks]
    self_send = self_send.reshape(energy_total, 1, owned_atoms, self_send.shape[-1])
    self_moved = lax.all_to_all(self_send, "energy", split_axis=0, concat_axis=1, tiled=True)
    self_moved = self_moved[..., lookup]
    self_local = jnp.transpose(self_moved.reshape(local_energies, slab_atoms, NO, NO), (0, 2, 3, 1))
    left_product = jnp.einsum(
        "eipa,epja->eija", green_blocks, self_local, preferred_element_type=jnp.float32
    ).astype(jnp.bfloat16)
    corrected = green_blocks.astype(jnp.float32) + jnp.einsum(
        "eipa,epja->eija", left_product, green_blocks, preferred_element_type=jnp.float32
    )
    corrected = corrected.astype(jnp.bfloat16)
    return (corrected, polarization)


def solution(mesh):
    return jax.shard_map(
        body,
        mesh=mesh,
        in_specs=(
            P("energy", None, None, "layer"),
            P(None, None, None, "layer"),
            P(None, None, None, "layer"),
            P(None, "layer"),
            P(),
        ),
        out_specs=(P("energy", None, None, "layer"), P(None, None, ("layer", "energy"))),
        check_vma=False,
    )
```

profile of v0, /device:TPU:0, one launch (start us, length us, event | category | flops | bytes accessed | tf_op | source)
XLA Modules:
  0.0 140.1 jit_solution(4632984540969071357)
XLA Ops:
  0.6 5.0 %collective-permute-start = (bf16[1,12,12,384]{3,2,1,0:T(8,128)(2,1)}, bf16[1,12,12,384]{3,2,1,0:T(8,128)(2,1)S(1)}, u32[]{:S(2)}, u32[]{:S(2)}) collective-permute-start(bf16[1,12,12,384]{3,2,1,0:T(8,128)(2,1)} %param.13), channel_id=1, source_target_pairs={{0,1},{1,2},{2,3},{4,5},{5,6},{6,7},{8,9},{9,10},{10,11},{12,13},{... | collective-permute-start | bytes 331784 | tf_op jit(solution)/shard_map/ppermute | solution.py:21
  5.7 1.3 collective-permute-start.1
  7.0 1.2 reshape.113
  9.5 0.8 copy.92
  10.3 4.9 %all-to-all-start.2 = ((bf16[1,8,48,78]{3,2,0,1:T(8,128)(2,1)}), bf16[1,8,48,78]{3,2,0,1:T(8,128)(2,1)S(1)}, u32[]{:S(2)}, u32[]{:S(2)}) async-start(bf16[1,8,48,78]{3,2,0,1:T(8,128)(2,1)} %copy.92), calls=%async_computation.2 | async-start | bytes 196608 | tf_op jit(solution)/shard_map/all_to_all | solution.py:82
  16.6 6.4 %copy.74 = bf16[12,12,4,384]{1,0,3,2:T(8,128)(2,1)} copy(bf16[12,12,4,384]{3,2,1,0:T(4,128)(2,1)} %param.14) | data formatting | bytes 884736 | tf_op args[1]
  23.0 12.2 %copy.76 = bf16[12,12,4,384]{1,0,2,3:T(8,128)(2,1)} copy(bf16[12,12,4,384]{3,2,1,0:T(4,128)(2,1)S(1)} %copy-done.1) | data formatting | bytes 884736 | tf_op args[1]
  35.2 1.2 constant_dynamic-slice_fusion.1
  36.5 5.5 %copy.72 = bf16[1,12,12,1152]{2,1,3,0:T(8,128)(2,1)} copy(bf16[1,12,12,1152]{3,2,1,0:T(8,128)(2,1)S(1)} %pad_maximum_fusion) | data formatting | bytes 663552 | tf_op jit(solution)/shard_map/concatenate | solution.py:19
  42.0 8.7 %gather_fusion = bf16[1536,12,12]{2,1,0:T(8,128)(2,1)} fusion(bf16[12,12,1152]{1,0,2:T(8,128)(2,1)} %bitcast.112, s32[2048]{0:T(1024)S(1)} %pad_clamp_fusion), kind=kCustom, calls=%fused_computation | custom fusion | bytes 890880 | tf_op jit(solution)/shard_map/jit(_take)/gather | solution.py:67
  50.7 13.1 %copy.73 = bf16[4,384,12,12]{2,3,1,0:T(8,128)(2,1)} copy(bf16[4,384,12,12]{3,2,1,0:T(8,128)(2,1)} %bitcast.111) | data formatting | bytes 884736 | tf_op jit(solution)/shard_map/jit(_take)/gather | solution.py:67
  63.8 7.0 %fusion.6 = f32[12,12,4,384]{0,1,3,2:T(8,128)S(1)} fusion(bf16[12,12,4,384]{1,0,3,2:T(8,128)(2,1)} %copy.74, bf16[4,384,12,12]{2,3,1,0:T(8,128)(2,1)} %copy.73, pred[4,384]{1,0:T(4,128)(4,1)S(1)} %compare_and_fusion), kind=kOutput, calls=%fused_computation.14 | convolution fusion | flops 5529600 | bytes 1771008 | tf_op jit(solution)/shard_map/ipka,epqka->eiqka/dot_general | solution.py:68
  70.9 13.4 %convert_bitcast_fusion = bf16[1,384,4,12,12]{4,3,2,1,0:T(8,128)(2,1)} fusion(bf16[12,12,4,384]{1,0,2,3:T(8,128)(2,1)} %copy.76, f32[12,12,4,384]{0,1,3,2:T(8,128)S(1)} %fusion.6), kind=kOutput, calls=%fused_computation.12 | convolution fusion | flops 32071680 | bytes 1769472 | tf_op jit(solution)/shard_map/eiqka,jqka->eakij/dot_general | solution.py:71
  84.3 7.9 %reshape.200 = bf16[8,48,4,144]{3,2,1,0:T(4,128)(2,1)S(1)} reshape(bf16[1,384,4,12,12]{4,3,2,1,0:T(8,128)(2,1)} %convert_bitcast_fusion) | data formatting | bytes 884736 | tf_op jit(solution)/shard_map/reshape | solution.py:74
  92.2 1.8 %copy.78 = bf16[8,48,4,144]{1,0,3,2:T(8,128)(2,1)S(1)} copy(bf16[8,48,4,144]{3,2,1,0:T(4,128)(2,1)S(1)} %reshape.200) | data formatting | bytes 884736 | tf_op jit(solution)/shard_map/reshape | solution.py:74
  94.7 1.5 %copy.79 = bf16[1,8,48,4,78]{4,2,3,0,1:T(8,128)(2,1)} copy(bf16[1,8,48,4,78]{2,1,3,4,0:T(8,128)(2,1)S(1)} %bitcast.116) | data formatting | bytes 479232 | tf_op jit(solution)/shard_map/gather | solution.py:78
  96.2 5.0 %all-to-all-start = ((bf16[1,8,48,4,78]{4,2,3,0,1:T(8,128)(2,1)}), bf16[1,8,48,4,78]{4,2,3,0,1:T(8,128)(2,1)S(1)}, u32[]{:S(2)}, u32[]{:S(2)}) async-start(bf16[1,8,48,4,78]{4,2,3,0,1:T(8,128)(2,1)} %copy.79), calls=%async_computation | async-start | bytes 786432 | tf_op jit(solution)/shard_map/all_to_all | solution.py:81
  101.5 2.2 %copy.91 = f32[1,12,12,384]{2,1,3,0:T(8,128)} copy(bf16[1,12,12,384]{3,2,1,0:T(8,128)(2,1)S(1)} %copy-done) | data formatting | bytes 331776 | tf_op jit(solution)/shard_map/convert_element_type | solution.py:111
  103.9 1.5 %copy.83 = f32[48,4,8,8]{3,2,1,0:T(8,128)} copy(f32[48,4,8,8]{0,3,1,2:T(8,128)S(1)} %fusion.16) | data formatting | bytes 98304 | tf_op jit(solution)/shard_map/add | solution.py:92
  105.4 1.4 %copy.88 = bf16[12,12,384]{1,0,2:T(8,128)(2,1)S(1)} copy(bf16[12,12,384]{2,1,0:T(8,128)(2,1)S(1)} %bitcast.115) | data formatting | bytes 221184 | tf_op jit(solution)/shard_map/reshape.22
  107.8 1.0 copy.104
  108.7 5.0 %all-to-all-done = bf16[1,8,48,4,78]{4,2,3,0,1:T(8,128)(2,1)S(1)} async-done(((bf16[1,8,48,4,78]{4,2,3,0,1:T(8,128)(2,1)}), bf16[1,8,48,4,78]{4,2,3,0,1:T(8,128)(2,1)S(1)}, u32[]{:S(2)}, u32[]{:S(2)}) %all-to-all-start) | async-done | bytes 239648 | tf_op jit(solution)/shard_map/all_to_all | solution.py:81
  114.2 1.0 gather_fusion.2
  115.2 1.7 %copy.82 = bf16[8,48,4,144]{3,0,2,1:T(8,128)(2,1)S(1)} copy(bf16[8,48,4,144]{1,0,2,3:T(8,128)(2,1)S(1)} %bitcast.113) | data formatting | bytes 884736 | tf_op jit(solution)/shard_map/gather | solution.py:84
  116.9 1.8 %fusion.15 = bf16[8,48,144]{2,0,1:T(8,128)(2,1)S(1)} fusion(bf16[8,48,4,144]{3,0,2,1:T(8,128)(2,1)S(1)} %copy.82, f32[48,4,8,8]{3,2,1,0:T(8,128)} %copy.83), kind=kOutput, calls=%fused_computation.23 | convolution fusion | flops 21288960 | bytes 602112 | tf_op jit(solution)/shard_map/akef,fakc->eac/dot_general | solution.py:93
  120.4 3.4 %all-to-all-start.1 = ((bf16[8,1,48,78]{3,2,1,0:T(8,128)(2,1)}), bf16[8,1,48,78]{3,2,1,0:T(8,128)(2,1)S(1)}, u32[]{:S(2)}, u32[]{:S(2)}) async-start(bf16[8,1,48,78]{3,2,1,0:T(8,128)(2,1)} %copy.85), calls=%async_computation.1 | async-start | bytes 196608 | tf_op jit(solution)/shard_map/all_to_all | solution.py:105
  123.8 2.7 %convolution_bitcast_fusion = f32[48,4,8,8]{2,3,1,0:T(8,128)S(1)} fusion(bf16[8,48,144,1]{2,0,3,1:T(8,128)(2,1)} %copy.104, bf16[8,48,4,144]{3,0,2,1:T(8,128)(2,1)S(1)} %copy.82), kind=kOutput, calls=%fused_computation.20 | convolution fusion | flops 3538944 | bytes 602112 | tf_op jit(solution)/shard_map/fakc,eac->akfe/dot_general | solution.py:96
  126.5 0.8 fusion.18
  128.1 2.0 %all-to-all-done.1 = bf16[8,1,48,78]{3,2,1,0:T(8,128)(2,1)S(1)} async-done(((bf16[8,1,48,78]{3,2,1,0:T(8,128)(2,1)}), bf16[8,1,48,78]{3,2,1,0:T(8,128)(2,1)S(1)}, u32[]{:S(2)}, u32[]{:S(2)}) %all-to-all-start.1) | async-done | bytes 59936 | tf_op jit(solution)/shard_map/all_to_all | solution.py:105
  131.2 1.3 copy.87
  132.5 4.7 %fusion.11 = bf16[1,12,12,384]{2,1,3,0:T(8,128)(2,1)} fusion(f32[1,12,12,384]{2,1,3,0:T(8,128)} %copy.91, bf16[12,12,384]{1,0,2:T(8,128)(2,1)S(1)} %copy.88, bf16[12,12,384]{0,1,2:T(8,128)(2,1)S(1)} %copy.87), kind=kOutput, calls=%fused_computation.16 | convolution fusion | flops 2820096 | bytes 552960 | tf_op jit(solution)/shard_map/eipa,epja->eija/dot_general | solution.py:111
  137.2 2.9 %copy.97 = bf16[1,12,12,384]{3,2,1,0:T(8,128)(2,1)} copy(bf16[1,12,12,384]{2,1,3,0:T(8,128)(2,1)} %fusion.11) | data formatting | bytes 221184
  (33 shorter events, 8.8 us)
Async XLA Ops:
  0.6 22.4 %copy-start.1 = (bf16[12,12,4,384]{3,2,1,0:T(4,128)(2,1)S(1)}, bf16[12,12,4,384]{3,2,1,0:T(4,128)(2,1)}, u32[]{:S(2)}) copy-start(bf16[12,12,4,384]{3,2,1,0:T(4,128)(2,1)} %param.14) | copy-start | bytes 1327108
  0.6 35.8 %collective-permute-start = (bf16[1,12,12,384]{3,2,1,0:T(8,128)(2,1)}, bf16[1,12,12,384]{3,2,1,0:T(8,128)(2,1)S(1)}, u32[]{:S(2)}, u32[]{:S(2)}) collective-permute-start(bf16[1,12,12,384]{3,2,1,0:T(8,128)(2,1)} %param.13), channel_id=1, source_target_pairs={{0,1},{1,2},{2,3},{4,5},{5,6},{6,7},{8,9},{9,10},{10,11},{12,13},{... | collective-permute-start | bytes 331784 | tf_op jit(solution)/shard_map/ppermute | solution.py:21
  5.7 30.8 %collective-permute-start.1 = (bf16[1,12,12,384]{3,2,1,0:T(8,128)(2,1)}, bf16[1,12,12,384]{3,2,1,0:T(8,128)(2,1)S(1)}, u32[]{:S(2)}, u32[]{:S(2)}) collective-permute-start(bf16[1,12,12,384]{3,2,1,0:T(8,128)(2,1)} %param.13), channel_id=1, source_target_pairs={{1,0},{2,1},{3,2},{5,4},{6,5},{7,6},{9,8},{10,9},{11,10},{13,12},{... | collective-permute-start | bytes 331784 | tf_op jit(solution)/shard_map/ppermute | solution.py:23
  10.3 85.9 %all-to-all-start.2 = ((bf16[1,8,48,78]{3,2,0,1:T(8,128)(2,1)}), bf16[1,8,48,78]{3,2,0,1:T(8,128)(2,1)S(1)}, u32[]{:S(2)}, u32[]{:S(2)}) async-start(bf16[1,8,48,78]{3,2,0,1:T(8,128)(2,1)} %copy.92), calls=%async_computation.2 | async-start | bytes 196608 | tf_op jit(solution)/shard_map/all_to_all | solution.py:82
  16.6 18.6 %copy-start.3 = (s32[48]{0:T(128)S(1)}, s32[48]{0:T(128)}, u32[]{:S(2)}) copy-start(s32[48]{0:T(128)} %param.17) | copy-start | bytes 580
  16.6 19.9 %copy-start = (bf16[1,12,12,384]{3,2,1,0:T(8,128)(2,1)S(1)}, bf16[1,12,12,384]{3,2,1,0:T(8,128)(2,1)}, u32[]{:S(2)}) copy-start(bf16[1,12,12,384]{3,2,1,0:T(8,128)(2,1)} %param.13) | copy-start | bytes 331780
  92.1 14.7 %copy-start.2 = (s32[144]{0:T(256)S(1)}, s32[144]{0:T(256)}, u32[]{:S(2)}) copy-start(s32[144]{0:T(256)} %constant.48) | copy-start | bytes 1732
  96.2 17.5 %all-to-all-start = ((bf16[1,8,48,4,78]{4,2,3,0,1:T(8,128)(2,1)}), bf16[1,8,48,4,78]{4,2,3,0,1:T(8,128)(2,1)S(1)}, u32[]{:S(2)}, u32[]{:S(2)}) async-start(bf16[1,8,48,4,78]{4,2,3,0,1:T(8,128)(2,1)} %copy.79), calls=%async_computation | async-start | bytes 786432 | tf_op jit(solution)/shard_map/all_to_all | solution.py:81
  120.4 9.6 %all-to-all-start.1 = ((bf16[8,1,48,78]{3,2,1,0:T(8,128)(2,1)}), bf16[8,1,48,78]{3,2,1,0:T(8,128)(2,1)S(1)}, u32[]{:S(2)}, u32[]{:S(2)}) async-start(bf16[8,1,48,78]{3,2,1,0:T(8,128)(2,1)} %copy.85), calls=%async_computation.1 | async-start | bytes 196608 | tf_op jit(solution)/shard_map/all_to_all | solution.py:105
where the time goes:
time: 142 us; the launch traced here: 140 us
  local copies, waits for them, and re-layouts  79.7 us (56%)
  matrix products  30.8 us (22%)
  starting transfers between devices  19.6 us (14%)
  waiting for transfers between devices  7 us (5%)
  other arithmetic  2.12 us (1%)
    unnamed x12, local copies, waits for them, and re-layouts  22.3 us
    gather x2, local copies, waits for them, and re-layouts, body(): gathered = jnp.take(window, neighbours, axis=3)  21.8 us
    dot_general x1, matrix products, body(): jnp.einsum('eiqka,jqka->eakij', first_product, coupling.astype(jnp.float3...  13.4 us
    reshape x2, local copies, waits for them, and re-layouts, body(): product.reshape(local_energies, energy_count, owned_atoms, NBR, entries)  9.66 us
    dot_general x1, matrix products, body(): jnp.einsum('ipka,epqka->eiqka', coupling, gathered, preferred_element_typ...  7.02 us
    concatenate x1, local copies, waits for them, and re-layouts, with_halo(): jnp.concatenate([lax.ppermute(tail, axis, [(i, (i + 1) % count) for i in...  5.53 us
    all_to_all x1, waiting for transfers between devices, body(): lax.all_to_all(product_send, 'energy', split_axis=1, concat_axis=0, tiled...  5.03 us
    all_to_all x1, starting transfers between devices, body(): lax.all_to_all(product_send, 'energy', split_axis=1, concat_axis=0, tiled...  5.02 us
  transfers between devices with their start and end apart: 5, of which 2 were waited for; matrix products, arithmetic and copies ran while one was open for 69% of the time, Pallas kernels for 0%

commit v1 on v0

v1 whole, which is shorter than its diff:
```python
import functools
import math

import jax
import jax.numpy as jnp
import numpy as np
from jax import lax
from jax.experimental import pallas as pl
from jax.experimental.pallas import tpu as pltpu
from jax.sharding import PartitionSpec as P

MESH = pl.DeviceIdType.MESH
LANES = 128
F32 = jnp.float32
BF16 = jnp.bfloat16


def offsets(order):
    return [p * order - p * (p - 1) // 2 for p in range(order)]


def expansion(order, row_stride, packed_rows):
    off = offsets(order)
    table = np.zeros((order * row_stride, packed_rows), np.float32)
    for p in range(order):
        for q in range(order):
            low, high = min(p, q), max(p, q)
            table[p * row_stride + q, off[low] + high - low] = 1.0
    return jnp.asarray(table, BF16)


def kernel(
    reach, shift_ref, green_ref, coup_ref, weight_ref, near_ref, e12_ref, e16_ref,
    out_ref, pol_ref,
    tri32, own, halo, gin, pout, pin, chunks, cin, c4, g3, pscr, g16, s16, l16, ab,
    halo_send, halo_recv, gin_send, gin_recv, part_send, part_recv, chunk_send, chunk_recv,
):
    order = green_ref.shape[0]
    atoms = green_ref.shape[2]
    nbr = near_ref.shape[0]
    freqs = shift_ref.shape[0]
    tiles = atoms // LANES
    packed = own.shape[0]
    pad = c4.shape[2]
    ne = lax.axis_size("energy")
    nl = lax.axis_size("layer")
    me = lax.axis_index("energy")
    layer = lax.axis_index("layer")
    share = atoms // ne
    off = offsets(order)

    barrier = pltpu.get_barrier_semaphore()
    for r in range(1, ne):
        pl.semaphore_signal(
            barrier, inc=1, device_id={"energy": lax.rem(me + r, ne), "layer": layer},
            device_id_type=MESH,
        )

    @pl.when(layer > 0)
    def _():
        pl.semaphore_signal(
            barrier, inc=1, device_id={"energy": me, "layer": layer - 1}, device_id_type=MESH
        )

    @pl.when(layer < nl - 1)
    def _():
        pl.semaphore_signal(
            barrier, inc=1, device_id={"energy": me, "layer": layer + 1}, device_id_type=MESH
        )

    tri32[...] = jnp.zeros_like(tri32)
    for p in range(order):
        tri32[off[p] : off[p] + order - p, :] = green_ref[p].astype(F32)[p:, :]
    own[...] = tri32[...].astype(BF16)

    @pl.when(layer == 0)
    def _():
        halo[0] = jnp.zeros((packed, atoms), BF16)

    @pl.when(layer == nl - 1)
    def _():
        halo[1] = jnp.zeros((packed, atoms), BF16)

    for d in range(1, reach + 1):

        @pl.when(me < d)
        def _():
            gin[d - 1] = jnp.zeros((packed, atoms), BF16)
            pin[2 * d - 2] = jnp.zeros((packed, atoms), BF16)

        @pl.when(me + d >= ne)
        def _():
            pin[2 * d - 1] = jnp.zeros((packed, atoms), BF16)

    pl.semaphore_wait(
        barrier, ne - 1 + (layer > 0).astype(jnp.int32) + (layer < nl - 1).astype(jnp.int32)
    )

    def remote(src, dst, send, recv, energy, row):
        return pltpu.make_async_remote_copy(
            src_ref=src, dst_ref=dst, send_sem=send, recv_sem=recv,
            device_id={"energy": energy, "layer": row}, device_id_type=MESH,
        )

    def halo_copy(side):
        row = layer + 1 if side == 0 else layer - 1
        return remote(own, halo.at[side], halo_send.at[side], halo_recv.at[side], me, row)

    def green_copy(d):
        return remote(
            own, gin.at[d - 1], gin_send.at[d - 1], gin_recv.at[d - 1], me + d, layer
        )

    def part_copy(slot, energy):
        return remote(
            pout.at[slot], pin.at[slot], part_send.at[slot], part_recv.at[slot], energy, layer
        )

    def chunk_copy(r):
        dest = lax.rem(me + r, ne)
        return remote(
            chunks.at[dest], cin.at[r], chunk_send.at[r], chunk_recv.at[r], dest, layer
        )

    has_above, has_below = layer < nl - 1, layer > 0

    @pl.when(has_above)
    def _():
        halo_copy(0).start()

    @pl.when(has_below)
    def _():
        halo_copy(1).start()

    for d in range(1, reach + 1):

        @pl.when(me + d < ne)
        def _():
            green_copy(d).start()

    for t in range(tiles):
        block = coup_ref[:, :, t * LANES : (t + 1) * LANES].astype(F32)
        c4[:, :, t * nbr : (t + 1) * nbr, :] = block.reshape(order, order, nbr, LANES)

    def add_weights(w, sums):
        shift = shift_ref[w]
        low, high = weight_ref[w], weight_ref[freqs + w]
        new = []
        for d in range(1, reach + 1):
            pick = jnp.where(shift == d, 1.0, 0.0).astype(F32)
            new += [sums[2 * d - 2] + pick * low, sums[2 * d - 1] + pick * high]
        return tuple(new)

    sums = lax.fori_loop(
        0, freqs, add_weights, tuple(jnp.zeros((nbr, atoms), F32) for _ in range(2 * reach))
    )
    for s in range(2 * reach):
        ab[s] = sums[s]

    row = lax.broadcasted_iota(jnp.int32, (atoms, atoms), 0)

    def pick_neighbours(k, block, start):
        hot = jnp.where(row == near_ref[k : k + 1, :] - start, 1.0, 0.0).astype(BF16)
        full = jnp.dot(e12_ref[...], block, preferred_element_type=F32).astype(BF16)
        found = jnp.dot(full, hot, preferred_element_type=F32)
        for t in range(tiles):
            g3[pl.ds(t * nbr + k, order * order, stride=pad), :] = found[
                :, t * LANES : (t + 1) * LANES
            ]

    for k in range(2, nbr):
        pick_neighbours(k, own[...], atoms)

    g16[...] = jnp.dot(e16_ref[...], own[...], preferred_element_type=F32).reshape(g16.shape)

    @pl.when(has_below)
    def _():
        halo_copy(0).wait_recv()

    @pl.when(has_above)
    def _():
        halo_copy(1).wait_recv()

    pick_neighbours(0, halo[0], 0)
    pick_neighbours(1, halo[1], 2 * atoms)

    last = off[-1] + 1
    pscr[last * pad :, :] = jnp.zeros(((packed - last) * pad, LANES), F32)
    for i in range(order):
        first = jnp.zeros((order, pad, LANES), F32)
        for p in range(order):
            block = g3[p * order * pad : (p + 1) * order * pad, :].reshape(order, pad, LANES)
            first = first + c4[i, p][None] * block
        total = first[0][None] * c4[i:, 0]
        for q in range(1, order):
            total = total + first[q][None] * c4[i:, q]
        total = total.astype(BF16).astype(F32)
        pscr[off[i] * pad : (off[i] + order - i) * pad, :] = total.reshape(-1, LANES)

    for d in range(1, reach + 1):

        @pl.when(me >= d)
        def _():
            green_copy(d).wait_recv()

    index = lax.broadcasted_iota(jnp.int32, (packed, LANES), 0)
    twice = jnp.full((packed, LANES), 2.0, F32)
    for p in range(order):
        twice = jnp.where(index == off[p], 1.0, twice)
    rows = [[] for _ in range(reach * nbr)]
    for t in range(tiles):
        lanes = slice(t * LANES, (t + 1) * LANES)
        greens = [gin[d, :, lanes].astype(F32) * twice for d in range(reach)]
        parts = [None] * (2 * reach)
        for k in range(nbr):
            value = pscr[pl.ds(t * nbr + k, packed, stride=pad), :]
            for s in range(2 * reach):
                term = ab[s, k : k + 1, lanes] * value
                parts[s] = term if parts[s] is None else parts[s] + term
            for d in range(reach):
                rows[d * nbr + k].append(jnp.sum(greens[d] * value, axis=0, keepdims=True))
        for s in range(2 * reach):
            pout[s, :, lanes] = parts[s].astype(BF16)

    for d in range(1, reach + 1):

        @pl.when(me + d < ne)
        def _():
            part_copy(2 * d - 2, me + d).start()

        @pl.when(me >= d)
        def _():
            part_copy(2 * d - 1, me - d).start()

    corr = jnp.concatenate([jnp.concatenate(r, axis=1) for r in rows], axis=0)
    width = chunks.shape[2]
    for e in range(ne):
        moved = corr if e == 0 else pltpu.roll(corr, atoms - e * share, 1)
        chunks[e] = moved[:, :width]
    for r in range(1, ne):
        chunk_copy(r).start()

    for d in range(1, reach + 1):

        @pl.when(me >= d)
        def _():
            part_copy(2 * d - 2, me).wait_recv()

        @pl.when(me + d < ne)
        def _():
            part_copy(2 * d - 1, me).wait_recv()

    sigma = pin[0].astype(F32)
    for s in range(1, 2 * reach):
        sigma = sigma + pin[s].astype(F32)
    s16[...] = jnp.dot(
        e16_ref[...], sigma.astype(BF16), preferred_element_type=F32
    ).reshape(s16.shape)

    def dyson(i, carry):
        left = g16[i, 0:1, :] * s16[0]
        for p in range(1, order):
            left = left + g16[i, p : p + 1, :] * s16[p]
        l16[...] = left.astype(BF16).astype(F32)
        total = g16[i]
        for p in range(order):
            total = total + l16[p : p + 1, :] * g16[p]
        out_ref[i] = total[:order].astype(BF16)
        return carry

    lax.fori_loop(0, order, dyson, 0)

    for r in range(1, ne):
        chunk_copy(r).wait_recv()
    summed = chunks[me]
    for r in range(1, ne):
        summed = summed + cin[r]
    summed = summed * (1.0 / (order * math.sqrt(ne)))
    summed = summed[:, :share]

    def expand(w, carry):
        shift = shift_ref[w]
        value = jnp.zeros((nbr, share), F32)
        for d in range(1, reach + 1):
            pick = jnp.where(shift == d, 1.0, 0.0).astype(F32)
            value = value + pick * summed[(d - 1) * nbr : d * nbr]
        pol_ref[w] = value
        return carry

    lax.fori_loop(0, freqs, expand, 0)

    @pl.when(has_above)
    def _():
        halo_copy(0).wait_send()

    @pl.when(has_below)
    def _():
        halo_copy(1).wait_send()

    for d in range(1, reach + 1):

        @pl.when(me + d < ne)
        def _():
            green_copy(d).wait_send()
            part_copy(2 * d - 2, me).wait_send()

        @pl.when(me >= d)
        def _():
            part_copy(2 * d - 1, me).wait_send()

    for r in range(1, ne):
        chunk_copy(r).wait_send()


def body(green_blocks, coupling, phonon_weights, neighbours, phonon_shifts):
    ne = lax.axis_size("energy")
    reach = max(ne // 4, 1)
    order = green_blocks.shape[1]
    atoms = green_blocks.shape[3]
    nbr = neighbours.shape[0]
    freqs = phonon_shifts.shape[0]
    tiles = atoms // LANES
    share = atoms // ne
    count = order * (order + 1) // 2
    packed = -(-count // 16) * 16
    pad = -(-(tiles * nbr) // 8) * 8
    rows = 16 * (-(-order // 16))
    width = -(-share // LANES) * LANES
    vmem = pl.BlockSpec(memory_space=pltpu.VMEM)
    smem = pl.BlockSpec(memory_space=pltpu.SMEM)
    dma = pltpu.SemaphoreType.DMA
    corrected, polarization = pl.pallas_call(
        functools.partial(kernel, reach),
        out_shape=(
            jax.ShapeDtypeStruct((order, order, atoms), BF16),
            jax.ShapeDtypeStruct((freqs, nbr, share), F32),
        ),
        in_specs=[smem, vmem, vmem, vmem, vmem, vmem, vmem],
        out_specs=(vmem, vmem),
        scratch_shapes=[
            pltpu.VMEM((packed, atoms), F32),
            pltpu.VMEM((packed, atoms), BF16),
            pltpu.VMEM((2, packed, atoms), BF16),
            pltpu.VMEM((reach, packed, atoms), BF16),
            pltpu.VMEM((2 * reach, packed, atoms), BF16),
            pltpu.VMEM((2 * reach, packed, atoms), BF16),
            pltpu.VMEM((ne, reach * nbr, width), F32),
            pltpu.VMEM((ne, reach * nbr, width), F32),
            pltpu.VMEM((order, order, pad, LANES), F32),
            pltpu.VMEM((order * order * pad, LANES), F32),
            pltpu.VMEM((packed * pad, LANES), F32),
            pltpu.VMEM((order, rows, atoms), F32),
            pltpu.VMEM((order, rows, atoms), F32),
            pltpu.VMEM((rows, atoms), F32),
            pltpu.VMEM((2 * reach, nbr, atoms), F32),
            dma((2,)), dma((2,)), dma((reach,)), dma((reach,)),
            dma((2 * reach,)), dma((2 * reach,)), dma((ne,)), dma((ne,)),
        ],
        compiler_params=pltpu.CompilerParams(collective_id=0, has_side_effects=True),
    )(
        phonon_shifts,
        green_blocks[0],
        coupling.reshape(order * order, nbr, atoms),
        phonon_weights.reshape(2 * freqs, nbr, atoms),
        neighbours,
        expansion(order, order, packed),
        expansion(order, rows, packed),
    )
    return corrected[None], polarization


def solution(mesh):
    return jax.shard_map(
        body,
        mesh=mesh,
        in_specs=(
            P("energy", None, None, "layer"),
            P(None, None, None, "layer"),
            P(None, None, None, "layer"),
            P(None, "layer"),
            P(),
        ),
        out_specs=(P("energy", None, None, "layer"), P(None, None, ("layer", "energy"))),
        check_vma=False,
    )
```

time: 142 us -> 23.2 us (0.16); the launches traced: 140 us -> 23.1 us
  local copies, waits for them, and re-layouts: 79.7 us -> 2.26 us
  matrix products: 30.8 us -> 0 us
  Pallas kernels: 0 us -> 20.2 us
  starting transfers between devices: 19.6 us -> 0 us
  waiting for transfers between devices: 7 us -> 0 us
  other arithmetic: 2.12 us -> 0 us
    gather x12 -> x0, local copies, waits for them, and re-layouts: 31.3 us -> none  [the longest x2 21.8 us: body(): gathered = jnp.take(window, neighbours, axis=3)]
    dot_general x8 -> x0, matrix products: 30.8 us -> none  [the longest x1 13.4 us: body(): jnp.einsum('eiqka,jqka->eakij', first_product, coupling.astype(jnp.float3...]
    pallas_call x0 -> x1, Pallas kernels: none -> 20.2 us  [body(): pl.pallas_call(functools.partial(kernel, reach), out_shape=(jax.ShapeDtyp...]
    unnamed x12 -> x4, local copies, waits for them, and re-layouts: 22.3 us -> 2.26 us
    all_to_all x3 -> x0, starting transfers between devices: 13.3 us -> none  [the longest x1 5.02 us: body(): lax.all_to_all(product_send, 'energy', split_axis=1, concat_axis=0, tiled...]
    reshape x5 -> x0, local copies, waits for them, and re-layouts: 11.9 us -> none  [the longest x2 9.66 us: body(): product.reshape(local_energies, energy_count, owned_atoms, NBR, entries)]
    all_to_all x3 -> x0, waiting for transfers between devices: 6.99 us -> none  [the longest x1 5.03 us: body(): lax.all_to_all(product_send, 'energy', split_axis=1, concat_axis=0, tiled...]
    ppermute x2 -> x0, starting transfers between devices: 6.31 us -> none  [the longest x1 5.01 us: with_halo(): lax.ppermute(tail, axis, [(i, (i + 1) % count) for i in range(ends)])]
  transfers between devices with their start and end apart: 5 -> 0, of which waited for: 2 -> 0; matrix products, arithmetic and copies ran while one was open for 69% -> 0% of each run, Pallas kernels for 0% -> 0%
where the time goes in v1:
time: 23.2 us; the launch traced here: 23.1 us
  Pallas kernels  20.2 us (87%)
  local copies, waits for them, and re-layouts  2.26 us (10%)
  between operations  0.65 us (3%)
    pallas_call x1, Pallas kernels, body(): pl.pallas_call(functools.partial(kernel, reach), out_shape=(jax.ShapeDtyp...  20.2 us
    unnamed x4, local copies, waits for them, and re-layouts  2.26 us

profile of v1, /device:TPU:0, one launch (start us, length us, event | category | flops | bytes accessed | tf_op | source)
XLA Modules:
  0.0 23.1 jit_solution(3188854251621243257)
XLA Ops:
  0.6 20.2 %shard_map.86 = (bf16[12,12,384]{2,1,0:T(8,128)(2,1)}, f32[48,4,48]{2,1,0:T(4,128)}) custom-call(s32[48]{0:T(128)} %shift_ref.1, bf16[12,12,384]{2,1,0:T(8,128)(2,1)} %bitcast.6, bf16[144,4,384]{2,1,0:T(4,128)(2,1)} %bitcast.5, f32[96,4,384]{2,1,0:T(4,128)} %bitcast.4, s32[4,384]{1,0:T(4,128)} %near_ref.1, bf16[144,80]{1,0:T(8,128)(2,1)} %constant.4.clone.e12_ref, ...), custom_call_target="tpu_custom_call" | custom-call | tf_op jit(solution)/shard_map/pallas_call | solution.py:332
  20.8 0.0 copy-start
  20.8 1.6 %copy.11 = bf16[1,12,12,384]{3,2,1,0:T(8,128)(2,1)} copy(bf16[1,12,12,384]{3,2,1,0:T(8,128)(2,1)} %bitcast.7) | data formatting | bytes 221184
  22.4 0.0 copy-done
  22.4 0.6 %copy.12 = f32[48,4,48]{2,1,0:T(4,128)} copy(f32[48,4,48]{2,1,0:T(4,128)S(1)} %copy-done) | data formatting | bytes 73728
Async XLA Ops:
  20.8 1.6 %copy-start = (f32[48,4,48]{2,1,0:T(4,128)S(1)}, f32[48,4,48]{2,1,0:T(4,128)}, u32[]{:S(2)}) copy-start(f32[48,4,48]{2,1,0:T(4,128)} %get-tuple-element.9) | copy-start | bytes 110596

commit v2 on v1

v2 whole, which is shorter than its diff:
```python
import functools
import math

import jax
import jax.numpy as jnp
import numpy as np
from jax import lax
from jax.experimental import pallas as pl
from jax.experimental.pallas import tpu as pltpu
from jax.sharding import PartitionSpec as P

MESH = pl.DeviceIdType.MESH
LANES = 128
F32 = jnp.float32
BF16 = jnp.bfloat16


def offsets(order):
    return [p * order - p * (p - 1) // 2 for p in range(order)]


def expansion(order, row_stride, packed_rows):
    off = offsets(order)
    table = np.zeros((order * row_stride, packed_rows), np.float32)
    for p in range(order):
        for q in range(order):
            low, high = min(p, q), max(p, q)
            table[p * row_stride + q, off[low] + high - low] = 1.0
    return jnp.asarray(table, BF16)


def kernel(
    reach, shift_ref, green_ref, coup_hbm, weight_hbm, near_ref, e12_ref,
    sig_ref, sum_ref,
    coup_ref, weight_ref, tri32, own, halo, gin, pout, pin, pacc, chunks, cin, c4, g3, pscr, ab,
    load_sem, halo_send, halo_recv, gin_send, gin_recv, part_send, part_recv,
    chunk_send, chunk_recv,
):
    order = green_ref.shape[0]
    atoms = green_ref.shape[2]
    nbr = near_ref.shape[0]
    freqs = shift_ref.shape[0]
    tiles = atoms // LANES
    packed = own.shape[0]
    pad = c4.shape[3]
    ne = lax.axis_size("energy")
    nl = lax.axis_size("layer")
    me = lax.axis_index("energy")
    layer = lax.axis_index("layer")
    share = atoms // ne
    off = offsets(order)
    groups = (tuple(range(2, nbr)), (0, 1))

    load_coup = pltpu.make_async_copy(coup_hbm, coup_ref, load_sem.at[0])
    load_weight = pltpu.make_async_copy(weight_hbm, weight_ref, load_sem.at[1])
    load_coup.start()
    load_weight.start()

    barrier = pltpu.get_barrier_semaphore()
    for r in range(1, ne):
        pl.semaphore_signal(
            barrier, inc=1, device_id={"energy": lax.rem(me + r, ne), "layer": layer},
            device_id_type=MESH,
        )

    @pl.when(layer > 0)
    def _():
        pl.semaphore_signal(
            barrier, inc=1, device_id={"energy": me, "layer": layer - 1}, device_id_type=MESH
        )

    @pl.when(layer < nl - 1)
    def _():
        pl.semaphore_signal(
            barrier, inc=1, device_id={"energy": me, "layer": layer + 1}, device_id_type=MESH
        )

    tri32[...] = jnp.zeros_like(tri32)
    for p in range(order):
        tri32[off[p] : off[p] + order - p, :] = green_ref[p].astype(F32)[p:, :]
    own[...] = tri32[...].astype(BF16)

    @pl.when(layer == 0)
    def _():
        halo[0] = jnp.zeros((packed, atoms), BF16)

    @pl.when(layer == nl - 1)
    def _():
        halo[1] = jnp.zeros((packed, atoms), BF16)

    for d in range(1, reach + 1):

        @pl.when(me < d)
        def _():
            gin[d - 1] = jnp.zeros((packed, atoms), BF16)
            pin[2 * d - 2] = jnp.zeros((packed, atoms), BF16)

        @pl.when(me + d >= ne)
        def _():
            pin[2 * d - 1] = jnp.zeros((packed, atoms), BF16)

    pl.semaphore_wait(
        barrier, ne - 1 + (layer > 0).astype(jnp.int32) + (layer < nl - 1).astype(jnp.int32)
    )

    def remote(src, dst, send, recv, energy, row):
        return pltpu.make_async_remote_copy(
            src_ref=src, dst_ref=dst, send_sem=send, recv_sem=recv,
            device_id={"energy": energy, "layer": row}, device_id_type=MESH,
        )

    def halo_copy(side):
        row = layer + 1 if side == 0 else layer - 1
        return remote(own, halo.at[side], halo_send.at[side], halo_recv.at[side], me, row)

    def green_copy(d):
        return remote(
            own, gin.at[d - 1], gin_send.at[d - 1], gin_recv.at[d - 1], me + d, layer
        )

    def part_copy(slot, energy):
        return remote(
            pout.at[slot], pin.at[slot], part_send.at[slot], part_recv.at[slot], energy, layer
        )

    def chunk_copy(r):
        dest = lax.rem(me + r, ne)
        return remote(
            chunks.at[dest], cin.at[r], chunk_send.at[r], chunk_recv.at[r], dest, layer
        )

    has_above, has_below = layer < nl - 1, layer > 0

    @pl.when(has_above)
    def _():
        halo_copy(0).start()

    @pl.when(has_below)
    def _():
        halo_copy(1).start()

    for d in range(1, reach + 1):

        @pl.when(me + d < ne)
        def _():
            green_copy(d).start()

    row = lax.broadcasted_iota(jnp.int32, (atoms, atoms), 0)

    def pick_neighbours(g, j, full, start):
        k, size = groups[g][j], len(groups[g])
        hot = jnp.where(row == near_ref[k : k + 1, :] - start, 1.0, 0.0).astype(BF16)
        found = jnp.dot(full, hot, preferred_element_type=F32)
        for t in range(tiles):
            g3[pl.ds(t * size + j, order * order, stride=pad), :] = found[
                :, t * LANES : (t + 1) * LANES
            ]

    def expanded(block):
        return jnp.dot(e12_ref[...], block, preferred_element_type=F32).astype(BF16)

    own_full = expanded(own[...])
    for j in range(len(groups[0])):
        pick_neighbours(0, j, own_full, atoms)

    load_coup.wait()
    for g, slots in enumerate(groups):
        size = len(slots)
        for t in range(tiles):
            block = coup_ref[:, :, t * LANES : (t + 1) * LANES].astype(F32)
            block = block.reshape(order, order, nbr, LANES)
            c4[g, :, :, t * size : (t + 1) * size, :] = block[
                :, :, slots[0] : slots[0] + size, :
            ]

    last = off[-1] + 1
    for g in range(2):
        pscr[g, last * pad :, :] = jnp.zeros(((packed - last) * pad, LANES), F32)

    def products(g):
        for i in range(0, order, 2):
            first = jnp.zeros((2, order, pad, LANES), F32)
            for p in range(order):
                block = g3[p * order * pad : (p + 1) * order * pad, :]
                block = block.reshape(order, pad, LANES)
                first = first + c4[g, i : i + 2, p][:, None] * block[None]
            total = first[:, 0][:, None] * c4[g, i:, 0][None]
            for q in range(1, order):
                total = total + first[:, q][:, None] * c4[g, i:, q][None]
            total = total.astype(BF16).astype(F32)
            for n in range(2):
                pscr[g, off[i + n] * pad : (off[i + n] + order - i - n) * pad, :] = total[
                    n, n:
                ].reshape(-1, LANES)

    products(0)

    load_weight.wait()

    def add_weights(w, sums):
        shift = shift_ref[w]
        low, high = weight_ref[w], weight_ref[freqs + w]
        new = []
        for d in range(1, reach + 1):
            pick = jnp.where(shift == d, 1.0, 0.0).astype(F32)
            new += [sums[2 * d - 2] + pick * low, sums[2 * d - 1] + pick * high]
        return tuple(new)

    sums = lax.fori_loop(
        0, freqs, add_weights, tuple(jnp.zeros((nbr, atoms), F32) for _ in range(2 * reach)),
        unroll=4,
    )
    for s in range(2 * reach):
        ab[s] = sums[s]

    def partials(g, t, s):
        slots, lanes = groups[g], slice(t * LANES, (t + 1) * LANES)
        total = None
        for j, k in enumerate(slots):
            value = pscr[g, pl.ds(t * len(slots) + j, packed, stride=pad), :]
            term = ab[s, k : k + 1, lanes] * value
            total = term if total is None else total + term
        return total

    for t in range(tiles):
        for s in range(2 * reach):
            pacc[s, :, t * LANES : (t + 1) * LANES] = partials(0, t, s)

    @pl.when(has_below)
    def _():
        halo_copy(0).wait_recv()

    @pl.when(has_above)
    def _():
        halo_copy(1).wait_recv()

    pick_neighbours(1, 0, expanded(halo[0]), 0)
    pick_neighbours(1, 1, expanded(halo[1]), 2 * atoms)
    products(1)

    for t in range(tiles):
        lanes = slice(t * LANES, (t + 1) * LANES)
        for s in range(2 * reach):
            pout[s, :, lanes] = (pacc[s, :, lanes] + partials(1, t, s)).astype(BF16)

    for d in range(1, reach + 1):

        @pl.when(me + d < ne)
        def _():
            part_copy(2 * d - 2, me + d).start()

        @pl.when(me >= d)
        def _():
            part_copy(2 * d - 1, me - d).start()

    for d in range(1, reach + 1):

        @pl.when(me >= d)
        def _():
            green_copy(d).wait_recv()

    index = lax.broadcasted_iota(jnp.int32, (packed, LANES), 0)
    twice = jnp.full((packed, LANES), 2.0, F32)
    for p in range(order):
        twice = jnp.where(index == off[p], 1.0, twice)
    rows = [[] for _ in range(reach * nbr)]
    for t in range(tiles):
        lanes = slice(t * LANES, (t + 1) * LANES)
        greens = [gin[d, :, lanes].astype(F32) * twice for d in range(reach)]
        for g, slots in enumerate(groups):
            for j, k in enumerate(slots):
                value = pscr[g, pl.ds(t * len(slots) + j, packed, stride=pad), :]
                for d in range(reach):
                    rows[d * nbr + k].append(jnp.sum(greens[d] * value, axis=0, keepdims=True))

    corr = jnp.concatenate([jnp.concatenate(r, axis=1) for r in rows], axis=0)
    width = chunks.shape[2]
    for e in range(ne):
        moved = corr if e == 0 else pltpu.roll(corr, atoms - e * share, 1)
        chunks[e] = moved[:, :width]
    for r in range(1, ne):
        chunk_copy(r).start()

    for d in range(1, reach + 1):

        @pl.when(me >= d)
        def _():
            part_copy(2 * d - 2, me).wait_recv()

        @pl.when(me + d < ne)
        def _():
            part_copy(2 * d - 1, me).wait_recv()

    sigma = pin[0].astype(F32)
    for s in range(1, 2 * reach):
        sigma = sigma + pin[s].astype(F32)
    sig_ref[...] = sigma.astype(BF16)

    for r in range(1, ne):
        chunk_copy(r).wait_recv()
    summed = chunks[me]
    for r in range(1, ne):
        summed = summed + cin[r]
    sum_ref[...] = summed * (1.0 / (order * math.sqrt(ne)))

    @pl.when(has_above)
    def _():
        halo_copy(0).wait_send()

    @pl.when(has_below)
    def _():
        halo_copy(1).wait_send()

    for d in range(1, reach + 1):

        @pl.when(me + d < ne)
        def _():
            green_copy(d).wait_send()
            part_copy(2 * d - 2, me).wait_send()

        @pl.when(me >= d)
        def _():
            part_copy(2 * d - 1, me).wait_send()

    for r in range(1, ne):
        chunk_copy(r).wait_send()


def finish(
    reach, shift_ref, green_ref, sig_ref, sum_ref, e16_ref, out_ref, pol_ref, g16, s16, l16
):
    order = green_ref.shape[0]
    nbr, share = pol_ref.shape[1:]
    freqs = shift_ref.shape[0]
    rows = g16.shape[1]
    s16[...] = jnp.dot(
        e16_ref[...], sig_ref[...], preferred_element_type=F32
    ).reshape(s16.shape)
    g16[...] = jnp.zeros_like(g16)
    for p in range(order):
        g16[p, :order, :] = green_ref[p].astype(F32)

    for i in range(0, order, 2):
        left = [g16[i + n, 0:1, :] * s16[0] for n in range(2)]
        for p in range(1, order):
            block = s16[p]
            left = [left[n] + g16[i + n, p : p + 1, :] * block for n in range(2)]
        for n in range(2):
            l16[i + n] = left[n].astype(BF16).astype(F32)
    for i in range(0, order, 2):
        total = [g16[i + n] for n in range(2)]
        for p in range(order):
            block = g16[p]
            total = [total[n] + l16[i + n, p : p + 1, :] * block for n in range(2)]
        for n in range(2):
            out_ref[i + n] = total[n][:order].astype(BF16)

    summed = sum_ref[:, :share]
    for w in range(freqs):
        shift = shift_ref[w]
        value = jnp.zeros((nbr, share), F32)
        for d in range(1, reach + 1):
            value = jnp.where(shift == d, summed[(d - 1) * nbr : d * nbr], value)
        pol_ref[w] = value


def body(green_blocks, coupling, phonon_weights, neighbours, phonon_shifts):
    ne = lax.axis_size("energy")
    reach = max(ne // 4, 1)
    order = green_blocks.shape[1]
    atoms = green_blocks.shape[3]
    nbr = neighbours.shape[0]
    freqs = phonon_shifts.shape[0]
    tiles = atoms // LANES
    share = atoms // ne
    count = order * (order + 1) // 2
    packed = -(-count // 16) * 16
    pad = -(-(tiles * max(nbr - 2, 2)) // 8) * 8
    rows = 16 * (-(-order // 16))
    width = -(-share // LANES) * LANES
    vmem = pl.BlockSpec(memory_space=pltpu.VMEM)
    smem = pl.BlockSpec(memory_space=pltpu.SMEM)
    hbm = pl.BlockSpec(memory_space=pl.ANY)
    dma = pltpu.SemaphoreType.DMA
    green = green_blocks[0]
    sigma, summed = pl.pallas_call(
        functools.partial(kernel, reach),
        out_shape=(
            jax.ShapeDtypeStruct((packed, atoms), BF16),
            jax.ShapeDtypeStruct((reach * nbr, width), F32),
        ),
        in_specs=[smem, vmem, hbm, hbm, vmem, vmem],
        out_specs=(vmem, vmem),
        scratch_shapes=[
            pltpu.VMEM((order * order, nbr, atoms), BF16),
            pltpu.VMEM((2 * freqs, nbr, atoms), F32),
            pltpu.VMEM((packed, atoms), F32),
            pltpu.VMEM((packed, atoms), BF16),
            pltpu.VMEM((2, packed, atoms), BF16),
            pltpu.VMEM((reach, packed, atoms), BF16),
            pltpu.VMEM((2 * reach, packed, atoms), BF16),
            pltpu.VMEM((2 * reach, packed, atoms), BF16),
            pltpu.VMEM((2 * reach, packed, atoms), F32),
            pltpu.VMEM((ne, reach * nbr, width), F32),
            pltpu.VMEM((ne, reach * nbr, width), F32),
            pltpu.VMEM((2, order, order, pad, LANES), F32),
            pltpu.VMEM((order * order * pad, LANES), F32),
            pltpu.VMEM((2, packed * pad, LANES), F32),
            pltpu.VMEM((2 * reach, nbr, atoms), F32),
            dma((2,)), dma((2,)), dma((2,)), dma((reach,)), dma((reach,)),
            dma((2 * reach,)), dma((2 * reach,)), dma((ne,)), dma((ne,)),
        ],
        compiler_params=pltpu.CompilerParams(
            collective_id=0, has_side_effects=True, vmem_limit_bytes=32 << 20
        ),
    )(
        phonon_shifts,
        green,
        coupling.reshape(order * order, nbr, atoms),
        phonon_weights.reshape(2 * freqs, nbr, atoms),
        neighbours,
        expansion(order, order, packed),
    )
    corrected, polarization = pl.pallas_call(
        functools.partial(finish, reach),
        out_shape=(
            jax.ShapeDtypeStruct((order, order, atoms), BF16),
            jax.ShapeDtypeStruct((freqs, nbr, share), F32),
        ),
        in_specs=[smem, vmem, vmem, vmem, vmem],
        out_specs=(vmem, vmem),
        scratch_shapes=[pltpu.VMEM((order, rows, atoms), F32)] * 3,
        compiler_params=pltpu.CompilerParams(vmem_limit_bytes=32 << 20),
    )(phonon_shifts, green, sigma, summed, expansion(order, rows, packed))
    return corrected[None], polarization


def solution(mesh):
    return jax.shard_map(
        body,
        mesh=mesh,
        in_specs=(
            P("energy", None, None, "layer"),
            P(None, None, None, "layer"),
            P(None, None, None, "layer"),
            P(None, "layer"),
            P(),
        ),
        out_specs=(P("energy", None, None, "layer"), P(None, None, ("layer", "energy"))),
        check_vma=False,
    )
```

time: 23.2 us -> 24.9 us (1.073)
  local copies, waits for them, and re-layouts: 2.26 us -> 5.1 us
  Pallas kernels: 20.2 us -> 18.8 us
    pallas_call x1, Pallas kernels: 20.2 us -> 16.9 us  [body(): pl.pallas_call(functools.partial(kernel, reach), out_shape=(jax.ShapeDtyp...]
    unnamed x4 -> x14, local copies, waits for them, and re-layouts: 2.26 us -> 5.1 us
    pallas_call x0 -> x1, Pallas kernels: none -> 1.9 us  [body(): pl.pallas_call(functools.partial(finish, reach), out_shape=(jax.ShapeDtyp...]
where the time goes in v2:
time: 24.9 us; the launch traced here: 24.5 us
  Pallas kernels  18.8 us (76%)
  local copies, waits for them, and re-layouts  5.1 us (20%)
  between operations  0.66 us (3%)
    pallas_call x1, Pallas kernels, body(): pl.pallas_call(functools.partial(kernel, reach), out_shape=(jax.ShapeDtyp...  16.9 us
    unnamed x14, local copies, waits for them, and re-layouts  5.1 us
    pallas_call x1, Pallas kernels, body(): pl.pallas_call(functools.partial(finish, reach), out_shape=(jax.ShapeDtyp...  1.9 us

profile of v2, /device:TPU:0, one launch (start us, length us, event | category | flops | bytes accessed | tf_op | source)
XLA Modules:
  0.0 24.5 jit_solution(4173295516319034670)
XLA Ops:
  0.6 0.0 copy-start.6
  0.6 0.6 %copy-done.6 = s32[48]{0:T(128)S(1)} copy-done((s32[48]{0:T(128)S(1)}, s32[48]{0:T(128)}, u32[]{:S(2)}) %copy-start.6) | copy-done | bytes 216
  1.3 0.0 copy-start
  1.3 0.9 %copy-done = bf16[1,12,12,384]{3,2,1,0:T(8,128)(2,1)S(1)} copy-done((bf16[1,12,12,384]{3,2,1,0:T(8,128)(2,1)S(1)}, bf16[1,12,12,384]{3,2,1,0:T(8,128)(2,1)}, u32[]{:S(2)}) %copy-start) | copy-done | bytes 110616
  2.2 0.0 copy-start.1
  2.2 1.1 %copy-done.1 = f32[2,48,4,384]{3,2,1,0:T(4,128)S(1)} copy-done((f32[2,48,4,384]{3,2,1,0:T(4,128)S(1)}, f32[2,48,4,384]{3,2,1,0:T(4,128)}, u32[]{:S(2)}) %copy-start.1) | copy-done | bytes 589848
  3.3 0.0 copy-start.2
  3.3 1.0 %copy-done.2 = bf16[12,12,4,384]{3,2,1,0:T(4,128)(2,1)S(1)} copy-done((bf16[12,12,4,384]{3,2,1,0:T(4,128)(2,1)S(1)}, bf16[12,12,4,384]{3,2,1,0:T(4,128)(2,1)}, u32[]{:S(2)}) %copy-start.2) | copy-done | bytes 442392
  4.3 0.0 copy-start.4
  4.3 0.8 %copy-done.4 = bf16[144,80]{1,0:T(8,128)(2,1)S(1)} copy-done((bf16[144,80]{1,0:T(8,128)(2,1)S(1)}, bf16[144,80]{1,0:T(8,128)(2,1)}, u32[]{:S(2)}) %copy-start.4) | copy-done | bytes 23064
  5.0 0.0 copy-start.5
  5.0 0.7 %copy-done.5 = s32[4,384]{1,0:T(4,128)S(1)} copy-done((s32[4,384]{1,0:T(4,128)S(1)}, s32[4,384]{1,0:T(4,128)}, u32[]{:S(2)}) %copy-start.5) | copy-done | bytes 6168
  5.7 0.0 copy-start.3
  5.7 16.9 %shard_map.86 = (bf16[80,384]{1,0:T(8,128)(2,1)S(1)}, f32[8,128]{1,0:T(8,128)S(1)}) custom-call(s32[48]{0:T(128)S(1)} %copy-done.6, bf16[12,12,384]{2,1,0:T(8,128)(2,1)S(1)} %bitcast.4, bf16[144,4,384]{2,1,0:T(4,128)(2,1)S(1)} %bitcast.7, f32[96,4,384]{2,1,0:T(4,128)S(1)} %bitcast.6, s32[4,384]{1,0:T(4,128)S(1)} %copy-done.5, bf16[144,80]{1,0:T(8,128)(2,1)S(1)} %copy-done.4), custom_call_target="tpu_custom_call" | custom-call | tf_op jit(solution)/shard_map/pallas_call | solution.py:386
  22.6 0.0 copy-done.3
  22.6 1.9 %shard_map.87 = (bf16[12,12,384]{2,1,0:T(8,128)(2,1)}, f32[48,4,48]{2,1,0:T(4,128)}) custom-call(s32[48]{0:T(128)S(1)} %copy-done.6, bf16[12,12,384]{2,1,0:T(8,128)(2,1)S(1)} %bitcast.5, bf16[80,384]{1,0:T(8,128)(2,1)S(1)} %get-tuple-element.6.sig_ref, f32[8,128]{1,0:T(8,128)S(1)} %get-tuple-element.7.sum_ref, bf16[192,80]{1,0:T(8,128)(2,1)S(1)} %copy-done.3), custom_call_target="tpu_custom_call" | custom-call | tf_op jit(solution)/shard_map/pallas_call | solution.py:424
Async XLA Ops:
  0.6 0.7 %copy-start.6 = (s32[48]{0:T(128)S(1)}, s32[48]{0:T(128)}, u32[]{:S(2)}) copy-start(s32[48]{0:T(128)} %shift_ref.3) | copy-start | bytes 580
  1.3 0.9 %copy-start = (bf16[1,12,12,384]{3,2,1,0:T(8,128)(2,1)S(1)}, bf16[1,12,12,384]{3,2,1,0:T(8,128)(2,1)}, u32[]{:S(2)}) copy-start(bf16[1,12,12,384]{3,2,1,0:T(8,128)(2,1)} %param.7) | copy-start | bytes 331780
  2.2 1.1 %copy-start.1 = (f32[2,48,4,384]{3,2,1,0:T(4,128)S(1)}, f32[2,48,4,384]{3,2,1,0:T(4,128)}, u32[]{:S(2)}) copy-start(f32[2,48,4,384]{3,2,1,0:T(4,128)} %param.9) | copy-start | bytes 1769476
  3.3 1.0 %copy-start.2 = (bf16[12,12,4,384]{3,2,1,0:T(4,128)(2,1)S(1)}, bf16[12,12,4,384]{3,2,1,0:T(4,128)(2,1)}, u32[]{:S(2)}) copy-start(bf16[12,12,4,384]{3,2,1,0:T(4,128)(2,1)} %param.8) | copy-start | bytes 1327108
  4.3 0.8 %copy-start.4 = (bf16[144,80]{1,0:T(8,128)(2,1)S(1)}, bf16[144,80]{1,0:T(8,128)(2,1)}, u32[]{:S(2)}) copy-start(bf16[144,80]{1,0:T(8,128)(2,1)} %constant.4.clone.e12_ref) | copy-start | bytes 69124
  5.0 0.7 %copy-start.5 = (s32[4,384]{1,0:T(4,128)S(1)}, s32[4,384]{1,0:T(4,128)}, u32[]{:S(2)}) copy-start(s32[4,384]{1,0:T(4,128)} %near_ref.1) | copy-start | bytes 18436
  5.7 16.9 %copy-start.3 = (bf16[192,80]{1,0:T(8,128)(2,1)S(1)}, bf16[192,80]{1,0:T(8,128)(2,1)}, u32[]{:S(2)}) copy-start(bf16[192,80]{1,0:T(8,128)(2,1)} %constant.5.clone.e16_ref) | copy-start | bytes 92164

commit v3 on v2

--- a/solution.py
+++ b/solution.py
@@ -30,9 +30,9 @@
 
 
 def kernel(
-    reach, shift_ref, green_ref, coup_hbm, weight_hbm, near_ref, e12_ref,
+    reach, shift_hbm, green_hbm, coup_hbm, weight_hbm, near_hbm, e12_hbm,
     sig_ref, sum_ref,
-    coup_ref, weight_ref, tri32, own, halo, gin, pout, pin, pacc, chunks, cin, c4, g3, pscr, ab,
+    shift_ref, green_ref, coup_ref, weight_ref, near_ref, e12_ref, tri32, own, halo, gin, pout, pin, pacc, chunks, cin, c4, g3, pscr, ab,
     load_sem, halo_send, halo_recv, gin_send, gin_recv, part_send, part_recv,
     chunk_send, chunk_recv,
 ):
@@ -51,10 +51,17 @@
     off = offsets(order)
     groups = (tuple(range(2, nbr)), (0, 1))
 
-    load_coup = pltpu.make_async_copy(coup_hbm, coup_ref, load_sem.at[0])
-    load_weight = pltpu.make_async_copy(weight_hbm, weight_ref, load_sem.at[1])
-    load_coup.start()
-    load_weight.start()
+    def load(n, src, dst):
+        copy = pltpu.make_async_copy(src, dst, load_sem.at[n])
+        copy.start()
+        return copy
+
+    load_green = load(0, green_hbm, green_ref)
+    load_near = load(1, near_hbm, near_ref)
+    load_e12 = load(2, e12_hbm, e12_ref)
+    load_coup = load(3, coup_hbm, coup_ref)
+    load_weight = load(4, weight_hbm, weight_ref)
+    load_shift = load(5, shift_hbm, shift_ref)
 
     barrier = pltpu.get_barrier_semaphore()
     for r in range(1, ne):
@@ -76,6 +83,7 @@
         )
 
     tri32[...] = jnp.zeros_like(tri32)
+    load_green.wait()
     for p in range(order):
         tri32[off[p] : off[p] + order - p, :] = green_ref[p].astype(F32)[p:, :]
     own[...] = tri32[...].astype(BF16)
@@ -93,11 +101,11 @@
         @pl.when(me < d)
         def _():
             gin[d - 1] = jnp.zeros((packed, atoms), BF16)
-            pin[2 * d - 2] = jnp.zeros((packed, atoms), BF16)
+            pin[2 * d - 2] = jnp.zeros(pin.shape[1:], BF16)
 
         @pl.when(me + d >= ne)
         def _():
-            pin[2 * d - 1] = jnp.zeros((packed, atoms), BF16)
+            pin[2 * d - 1] = jnp.zeros(pin.shape[1:], BF16)
 
     pl.semaphore_wait(
         barrier, ne - 1 + (layer > 0).astype(jnp.int32) + (layer < nl - 1).astype(jnp.int32)
@@ -118,9 +126,10 @@
             own, gin.at[d - 1], gin_send.at[d - 1], gin_recv.at[d - 1], me + d, layer
         )
 
-    def part_copy(slot, energy):
+    def part_copy(slot, t, energy):
         return remote(
-            pout.at[slot], pin.at[slot], part_send.at[slot], part_recv.at[slot], energy, layer
+            pout.at[slot, t], pin.at[slot, t], part_send.at[slot, t], part_recv.at[slot, t],
+            energy, layer,
         )
 
     def chunk_copy(r):
@@ -159,6 +168,8 @@
     def expanded(block):
         return jnp.dot(e12_ref[...], block, preferred_element_type=F32).astype(BF16)
 
+    load_near.wait()
+    load_e12.wait()
     own_full = expanded(own[...])
     for j in range(len(groups[0])):
         pick_neighbours(0, j, own_full, atoms)
@@ -196,6 +207,7 @@
     products(0)
 
     load_weight.wait()
+    load_shift.wait()
 
     def add_weights(w, sums):
         shift = shift_ref[w]
@@ -224,34 +236,7 @@
 
     for t in range(tiles):
         for s in range(2 * reach):
-            pacc[s, :, t * LANES : (t + 1) * LANES] = partials(0, t, s)
-
-    @pl.when(has_below)
-    def _():
-        halo_copy(0).wait_recv()
-
-    @pl.when(has_above)
-    def _():
-        halo_copy(1).wait_recv()
-
-    pick_neighbours(1, 0, expanded(halo[0]), 0)
-    pick_neighbours(1, 1, expanded(halo[1]), 2 * atoms)
-    products(1)
-
-    for t in range(tiles):
-        lanes = slice(t * LANES, (t + 1) * LANES)
-        for s in range(2 * reach):
-            pout[s, :, lanes] = (pacc[s, :, lanes] + partials(1, t, s)).astype(BF16)
-
-    for d in range(1, reach + 1):
-
-        @pl.when(me + d < ne)
-        def _():
-            part_copy(2 * d - 2, me + d).start()
-
-        @pl.when(me >= d)
-        def _():
-            part_copy(2 * d - 1, me - d).start()
+            pacc[s, t] = partials(0, t, s)
 
     for d in range(1, reach + 1):
 
@@ -263,16 +248,33 @@
     twice = jnp.full((packed, LANES), 2.0, F32)
     for p in range(order):
         twice = jnp.where(index == off[p], 1.0, twice)
-    rows = [[] for _ in range(reach * nbr)]
-    for t in range(tiles):
-        lanes = slice(t * LANES, (t + 1) * LANES)
-        greens = [gin[d, :, lanes].astype(F32) * twice for d in range(reach)]
-        for g, slots in enumerate(groups):
+    rows = [[None] * tiles for _ in range(reach * nbr)]
+
+    def correlate(g):
+        slots = groups[g]
+        for t in range(tiles):
+            lanes = slice(t * LANES, (t + 1) * LANES)
+            greens = [gin[d, :, lanes].astype(F32) * twice for d in range(reach)]
             for j, k in enumerate(slots):
                 value = pscr[g, pl.ds(t * len(slots) + j, packed, stride=pad), :]
                 for d in range(reach):
-                    rows[d * nbr + k].append(jnp.sum(greens[d] * value, axis=0, keepdims=True))
-
+                    rows[d * nbr + k][t] = jnp.sum(greens[d] * value, axis=0, keepdims=True)
+
+    correlate(0)
+
+    @pl.when(has_below)
+    def _():
+        halo_copy(0).wait_recv()
+
+    @pl.when(has_above)
+    def _():
+        halo_copy(1).wait_recv()
+
+    pick_neighbours(1, 0, expanded(halo[0]), 0)
+    pick_neighbours(1, 1, expanded(halo[1]), 2 * atoms)
+    products(1)
+
+    correlate(1)
     corr = jnp.concatenate([jnp.concatenate(r, axis=1) for r in rows], axis=0)
     width = chunks.shape[2]
     for e in range(ne):
@@ -281,20 +283,34 @@
     for r in range(1, ne):
         chunk_copy(r).start()
 
-    for d in range(1, reach + 1):
-
-        @pl.when(me >= d)
-        def _():
-            part_copy(2 * d - 2, me).wait_recv()
-
-        @pl.when(me + d < ne)
-        def _():
-            part_copy(2 * d - 1, me).wait_recv()
-
-    sigma = pin[0].astype(F32)
-    for s in range(1, 2 * reach):
-        sigma = sigma + pin[s].astype(F32)
-    sig_ref[...] = sigma.astype(BF16)
+    for t in range(tiles):
+        for s in range(2 * reach):
+            pout[s, t] = (pacc[s, t] + partials(1, t, s)).astype(BF16)
+        for d in range(1, reach + 1):
+
+            @pl.when(me + d < ne)
+            def _():
+                part_copy(2 * d - 2, t, me + d).start()
+
+            @pl.when(me >= d)
+            def _():
+                part_copy(2 * d - 1, t, me - d).start()
+
+    for t in range(tiles):
+        for d in range(1, reach + 1):
+
+            @pl.when(me >= d)
+            def _():
+                part_copy(2 * d - 2, t, me).wait_recv()
+
+            @pl.when(me + d < ne)
+            def _():
+                part_copy(2 * d - 1, t, me).wait_recv()
+
+        sigma = pin[0, t].astype(F32)
+        for s in range(1, 2 * reach):
+            sigma = sigma + pin[s, t].astype(F32)
+        sig_ref[:, t * LANES : (t + 1) * LANES] = sigma.astype(BF16)
 
     for r in range(1, ne):
         chunk_copy(r).wait_recv()
@@ -316,11 +332,13 @@
         @pl.when(me + d < ne)
         def _():
             green_copy(d).wait_send()
-            part_copy(2 * d - 2, me).wait_send()
+            for t in range(tiles):
+                part_copy(2 * d - 2, t, me).wait_send()
 
         @pl.when(me >= d)
         def _():
-            part_copy(2 * d - 1, me).wait_send()
+            for t in range(tiles):
+                part_copy(2 * d - 1, t, me).wait_send()
 
     for r in range(1, ne):
         chunk_copy(r).wait_send()
@@ -380,7 +398,7 @@
     width = -(-share // LANES) * LANES
     vmem = pl.BlockSpec(memory_space=pltpu.VMEM)
     smem = pl.BlockSpec(memory_space=pltpu.SMEM)
-    hbm = pl.BlockSpec(memory_space=pl.ANY)
+    hbm = pl.BlockSpec(memory_space=pltpu.HBM)
     dma = pltpu.SemaphoreType.DMA
     green = green_blocks[0]
     sigma, summed = pl.pallas_call(
@@ -389,29 +407,33 @@
             jax.ShapeDtypeStruct((packed, atoms), BF16),
             jax.ShapeDtypeStruct((reach * nbr, width), F32),
         ),
-        in_specs=[smem, vmem, hbm, hbm, vmem, vmem],
+        in_specs=[hbm] * 6,
         out_specs=(vmem, vmem),
         scratch_shapes=[
+            pltpu.SMEM((freqs,), jnp.int32),
+            pltpu.VMEM((order, order, atoms), BF16),
             pltpu.VMEM((order * order, nbr, atoms), BF16),
             pltpu.VMEM((2 * freqs, nbr, atoms), F32),
+            pltpu.VMEM((nbr, atoms), jnp.int32),
+            pltpu.VMEM((order * order, packed), BF16),
             pltpu.VMEM((packed, atoms), F32),
             pltpu.VMEM((packed, atoms), BF16),
             pltpu.VMEM((2, packed, atoms), BF16),
             pltpu.VMEM((reach, packed, atoms), BF16),
-            pltpu.VMEM((2 * reach, packed, atoms), BF16),
-            pltpu.VMEM((2 * reach, packed, atoms), BF16),
-            pltpu.VMEM((2 * reach, packed, atoms), F32),
+            pltpu.VMEM((2 * reach, tiles, packed, LANES), BF16),
+            pltpu.VMEM((2 * reach, tiles, packed, LANES), BF16),
+            pltpu.VMEM((2 * reach, tiles, packed, LANES), F32),
             pltpu.VMEM((ne, reach * nbr, width), F32),
             pltpu.VMEM((ne, reach * nbr, width), F32),
             pltpu.VMEM((2, order, order, pad, LANES), F32),
             pltpu.VMEM((order * order * pad, LANES), F32),
             pltpu.VMEM((2, packed * pad, LANES), F32),
             pltpu.VMEM((2 * reach, nbr, atoms), F32),
-            dma((2,)), dma((2,)), dma((2,)), dma((reach,)), dma((reach,)),
-            dma((2 * reach,)), dma((2 * reach,)), dma((ne,)), dma((ne,)),
+            dma((6,)), dma((2,)), dma((2,)), dma((reach,)), dma((reach,)),
+            dma((2 * reach, tiles)), dma((2 * reach, tiles)), dma((ne,)), dma((ne,)),
         ],
         compiler_params=pltpu.CompilerParams(
-            collective_id=0, has_side_effects=True, vmem_limit_bytes=32 << 20
+            collective_id=0, has_side_effects=True, vmem_limit_bytes=67043328
         ),
     )(
         phonon_shifts,
@@ -430,7 +452,7 @@
         in_specs=[smem, vmem, vmem, vmem, vmem],
         out_specs=(vmem, vmem),
         scratch_shapes=[pltpu.VMEM((order, rows, atoms), F32)] * 3,
-        compiler_params=pltpu.CompilerParams(vmem_limit_bytes=32 << 20),
+        compiler_params=pltpu.CompilerParams(vmem_limit_bytes=67043328),
     )(phonon_shifts, green, sigma, summed, expansion(order, rows, packed))
     return corrected[None], polarization
 

time: 24.9 us -> 19.8 us (0.80)
  local copies, waits for them, and re-layouts: 5.1 us -> 0 us
    unnamed x14 -> x0, local copies, waits for them, and re-layouts: 5.1 us -> none
    pallas_call x1, Pallas kernels: 1.9 us -> 2.31 us  [body(): pl.pallas_call(functools.partial(finish, reach), out_shape=(jax.ShapeDtyp...]
where the time goes in v3:
time: 19.8 us; the launch traced here: 19.7 us
  Pallas kernels  19 us (96%)
  between operations  0.64 us (3%)
    pallas_call x1, Pallas kernels, body(): pl.pallas_call(functools.partial(kernel, reach), out_shape=(jax.ShapeDtyp...  16.7 us
    pallas_call x1, Pallas kernels, body(): pl.pallas_call(functools.partial(finish, reach), out_shape=(jax.ShapeDtyp...  2.31 us

profile of v3, /device:TPU:0, one launch (start us, length us, event | category | flops | bytes accessed | tf_op | source)
XLA Modules:
  0.0 19.7 jit_solution(12561273892747072237)
XLA Ops:
  0.6 16.7 %shard_map.86 = (bf16[80,384]{1,0:T(8,128)(2,1)}, f32[8,128]{1,0:T(8,128)}) custom-call(s32[48]{0:T(128)} %shift_ref.1, bf16[12,12,384]{2,1,0:T(8,128)(2,1)} %bitcast.4, bf16[144,4,384]{2,1,0:T(4,128)(2,1)} %bitcast.7, f32[96,4,384]{2,1,0:T(4,128)} %bitcast.6, s32[4,384]{1,0:T(4,128)} %near_hbm.1, bf16[144,80]{1,0:T(8,128)(2,1)} %constant.4.clone.e12_hbm), custom_call_target="tpu_custom_call" | custom-call | tf_op jit(solution)/shard_map/pallas_call | solution.py:404
  17.3 2.3 %shard_map.87 = (bf16[12,12,384]{2,1,0:T(8,128)(2,1)}, f32[48,4,48]{2,1,0:T(4,128)}) custom-call(s32[48]{0:T(128)} %shift_ref.1, bf16[12,12,384]{2,1,0:T(8,128)(2,1)} %bitcast.5, bf16[80,384]{1,0:T(8,128)(2,1)} %get-tuple-element.6.sig_ref, f32[8,128]{1,0:T(8,128)} %get-tuple-element.7.sum_ref, bf16[192,80]{1,0:T(8,128)(2,1)} %constant.5.clone.e16_ref), custom_call_target="tpu_custom_call" | custom-call | tf_op jit(solution)/shard_map/pallas_call | solution.py:446

commit v4 on v3

--- a/solution.py
+++ b/solution.py
@@ -17,6 +17,17 @@
 
 def offsets(order):
     return [p * order - p * (p - 1) // 2 for p in range(order)]
+
+
+def segments(order, packed):
+    plan, start, first = [], 0, 0
+    for i in range(0, order, 2):
+        done = sum(order - n for n in range(i + 2))
+        stop = packed if i + 2 >= order else done // 16 * 16
+        if stop - start >= 32 or stop == packed:
+            plan.append((start, stop, first, i + 2))
+            start, first = stop, i + 2
+    return plan
 
 
 def expansion(order, row_stride, packed_rows):
@@ -32,7 +43,7 @@
 def kernel(
     reach, shift_hbm, green_hbm, coup_hbm, weight_hbm, near_hbm, e12_hbm,
     sig_ref, sum_ref,
-    shift_ref, green_ref, coup_ref, weight_ref, near_ref, e12_ref, tri32, own, halo, gin, pout, pin, pacc, chunks, cin, c4, g3, pscr, ab,
+    shift_ref, green_ref, coup_ref, weight_ref, near_ref, e12_ref, tri32, own, halo, gin, pout, pin, pacc, hots, chunks, cin, c4, g3, pscr, ab,
     load_sem, halo_send, halo_recv, gin_send, gin_recv, part_send, part_recv,
     chunk_send, chunk_recv,
 ):
@@ -49,6 +60,7 @@
     layer = lax.axis_index("layer")
     share = atoms // ne
     off = offsets(order)
+    plan = segments(order, packed)
     groups = (tuple(range(2, nbr)), (0, 1))
 
     def load(n, src, dst):
@@ -126,10 +138,12 @@
             own, gin.at[d - 1], gin_send.at[d - 1], gin_recv.at[d - 1], me + d, layer
         )
 
-    def part_copy(slot, t, energy):
+    def part_copy(slot, n, energy):
+        start, stop, _, _ = plan[n]
+        rows = pl.ds(start, stop - start)
         return remote(
-            pout.at[slot, t], pin.at[slot, t], part_send.at[slot, t], part_recv.at[slot, t],
-            energy, layer,
+            pout.at[slot, rows], pin.at[slot, rows], part_send.at[slot, n],
+            part_recv.at[slot, n], energy, layer,
         )
 
     def chunk_copy(r):
@@ -156,9 +170,11 @@
 
     row = lax.broadcasted_iota(jnp.int32, (atoms, atoms), 0)
 
-    def pick_neighbours(g, j, full, start):
-        k, size = groups[g][j], len(groups[g])
-        hot = jnp.where(row == near_ref[k : k + 1, :] - start, 1.0, 0.0).astype(BF16)
+    def one_hot(k, start):
+        return jnp.where(row == near_ref[k : k + 1, :] - start, 1.0, 0.0).astype(BF16)
+
+    def pick_neighbours(g, j, full, hot):
+        size = len(groups[g])
         found = jnp.dot(full, hot, preferred_element_type=F32)
         for t in range(tiles):
             g3[pl.ds(t * size + j, order * order, stride=pad), :] = found[
@@ -172,7 +188,9 @@
     load_e12.wait()
     own_full = expanded(own[...])
     for j in range(len(groups[0])):
-        pick_neighbours(0, j, own_full, atoms)
+        pick_neighbours(0, j, own_full, one_hot(groups[0][j], atoms))
+    hots[0] = one_hot(0, 0)
+    hots[1] = one_hot(1, 2 * atoms)
 
     load_coup.wait()
     for g, slots in enumerate(groups):
@@ -188,8 +206,8 @@
     for g in range(2):
         pscr[g, last * pad :, :] = jnp.zeros(((packed - last) * pad, LANES), F32)
 
-    def products(g):
-        for i in range(0, order, 2):
+    def products(g, start, stop):
+        for i in range(start, stop, 2):
             first = jnp.zeros((2, order, pad, LANES), F32)
             for p in range(order):
                 block = g3[p * order * pad : (p + 1) * order * pad, :]
@@ -204,7 +222,7 @@
                     n, n:
                 ].reshape(-1, LANES)
 
-    products(0)
+    products(0, 0, order)
 
     load_weight.wait()
     load_shift.wait()
@@ -225,18 +243,21 @@
     for s in range(2 * reach):
         ab[s] = sums[s]
 
-    def partials(g, t, s):
-        slots, lanes = groups[g], slice(t * LANES, (t + 1) * LANES)
+    def rows_of(g, t, j, start, stop):
+        at = start * pad + t * len(groups[g]) + j
+        return pscr[g, pl.ds(at, stop - start, stride=pad), :]
+
+    def partials(g, t, s, start, stop):
+        lanes = slice(t * LANES, (t + 1) * LANES)
         total = None
-        for j, k in enumerate(slots):
-            value = pscr[g, pl.ds(t * len(slots) + j, packed, stride=pad), :]
-            term = ab[s, k : k + 1, lanes] * value
+        for j, k in enumerate(groups[g]):
+            term = ab[s, k : k + 1, lanes] * rows_of(g, t, j, start, stop)
             total = term if total is None else total + term
         return total
 
     for t in range(tiles):
         for s in range(2 * reach):
-            pacc[s, t] = partials(0, t, s)
+            pacc[s, :, t * LANES : (t + 1) * LANES] = partials(0, t, s, 0, packed)
 
     for d in range(1, reach + 1):
 
@@ -250,17 +271,20 @@
         twice = jnp.where(index == off[p], 1.0, twice)
     rows = [[None] * tiles for _ in range(reach * nbr)]
 
-    def correlate(g):
-        slots = groups[g]
+    def correlate(g, start, stop):
         for t in range(tiles):
             lanes = slice(t * LANES, (t + 1) * LANES)
-            greens = [gin[d, :, lanes].astype(F32) * twice for d in range(reach)]
-            for j, k in enumerate(slots):
-                value = pscr[g, pl.ds(t * len(slots) + j, packed, stride=pad), :]
+            greens = [
+                gin[d, start:stop, lanes].astype(F32) * twice[start:stop] for d in range(reach)
+            ]
+            for j, k in enumerate(groups[g]):
+                value = rows_of(g, t, j, start, stop)
                 for d in range(reach):
-                    rows[d * nbr + k][t] = jnp.sum(greens[d] * value, axis=0, keepdims=True)
-
-    correlate(0)
+                    term = jnp.sum(greens[d] * value, axis=0, keepdims=True)
+                    old = rows[d * nbr + k][t]
+                    rows[d * nbr + k][t] = term if old is None else old + term
+
+    correlate(0, 0, packed)
 
     @pl.when(has_below)
     def _():
@@ -270,47 +294,50 @@
     def _():
         halo_copy(1).wait_recv()
 
-    pick_neighbours(1, 0, expanded(halo[0]), 0)
-    pick_neighbours(1, 1, expanded(halo[1]), 2 * atoms)
-    products(1)
-
-    correlate(1)
-    corr = jnp.concatenate([jnp.concatenate(r, axis=1) for r in rows], axis=0)
+    pick_neighbours(1, 0, expanded(halo[0]), hots[0])
+    pick_neighbours(1, 1, expanded(halo[1]), hots[1])
     width = chunks.shape[2]
-    for e in range(ne):
-        moved = corr if e == 0 else pltpu.roll(corr, atoms - e * share, 1)
-        chunks[e] = moved[:, :width]
-    for r in range(1, ne):
-        chunk_copy(r).start()
-
-    for t in range(tiles):
-        for s in range(2 * reach):
-            pout[s, t] = (pacc[s, t] + partials(1, t, s)).astype(BF16)
+
+    for n, (start, stop, first, final) in enumerate(plan):
+        products(1, first, final)
+        correlate(1, start, stop)
+        if stop == packed:
+            corr = jnp.concatenate([jnp.concatenate(r, axis=1) for r in rows], axis=0)
+            for e in range(ne):
+                moved = corr if e == 0 else pltpu.roll(corr, atoms - e * share, 1)
+                chunks[e] = moved[:, :width]
+            for r in range(1, ne):
+                chunk_copy(r).start()
+        for t in range(tiles):
+            lanes = slice(t * LANES, (t + 1) * LANES)
+            for s in range(2 * reach):
+                total = pacc[s, start:stop, lanes] + partials(1, t, s, start, stop)
+                pout[s, start:stop, lanes] = total.astype(BF16)
         for d in range(1, reach + 1):
 
             @pl.when(me + d < ne)
             def _():
-                part_copy(2 * d - 2, t, me + d).start()
+                part_copy(2 * d - 2, n, me + d).start()
 
             @pl.when(me >= d)
             def _():
-                part_copy(2 * d - 1, t, me - d).start()
-
-    for t in range(tiles):
+                part_copy(2 * d - 1, n, me - d).start()
+
+    for n, (start, stop, _, _) in enumerate(plan):
         for d in range(1, reach + 1):
 
             @pl.when(me >= d)
             def _():
-                part_copy(2 * d - 2, t, me).wait_recv()
+                part_copy(2 * d - 2, n, me).wait_recv()
 
             @pl.when(me + d < ne)
             def _():
-                part_copy(2 * d - 1, t, me).wait_recv()
-
-        sigma = pin[0, t].astype(F32)
+                part_copy(2 * d - 1, n, me).wait_recv()
+
+        sigma = pin[0, start:stop].astype(F32)
         for s in range(1, 2 * reach):
-            sigma = sigma + pin[s, t].astype(F32)
-        sig_ref[:, t * LANES : (t + 1) * LANES] = sigma.astype(BF16)
+            sigma = sigma + pin[s, start:stop].astype(F32)
+        sig_ref[start:stop, :] = sigma.astype(BF16)
 
     for r in range(1, ne):
         chunk_copy(r).wait_recv()
@@ -332,13 +359,13 @@
         @pl.when(me + d < ne)
         def _():
             green_copy(d).wait_send()
-            for t in range(tiles):
-                part_copy(2 * d - 2, t, me).wait_send()
+            for n in range(len(plan)):
+                part_copy(2 * d - 2, n, me).wait_send()
 
         @pl.when(me >= d)
         def _():
-            for t in range(tiles):
-                part_copy(2 * d - 1, t, me).wait_send()
+            for n in range(len(plan)):
+                part_copy(2 * d - 1, n, me).wait_send()
 
     for r in range(1, ne):
         chunk_copy(r).wait_send()
@@ -396,6 +423,7 @@
     pad = -(-(tiles * max(nbr - 2, 2)) // 8) * 8
     rows = 16 * (-(-order // 16))
     width = -(-share // LANES) * LANES
+    parts = len(segments(order, packed))
     vmem = pl.BlockSpec(memory_space=pltpu.VMEM)
     smem = pl.BlockSpec(memory_space=pltpu.SMEM)
     hbm = pl.BlockSpec(memory_space=pltpu.HBM)
@@ -420,9 +448,10 @@
             pltpu.VMEM((packed, atoms), BF16),
             pltpu.VMEM((2, packed, atoms), BF16),
             pltpu.VMEM((reach, packed, atoms), BF16),
-            pltpu.VMEM((2 * reach, tiles, packed, LANES), BF16),
-            pltpu.VMEM((2 * reach, tiles, packed, LANES), BF16),
-            pltpu.VMEM((2 * reach, tiles, packed, LANES), F32),
+            pltpu.VMEM((2 * reach, packed, atoms), BF16),
+            pltpu.VMEM((2 * reach, packed, atoms), BF16),
+            pltpu.VMEM((2 * reach, packed, atoms), F32),
+            pltpu.VMEM((2, atoms, atoms), BF16),
             pltpu.VMEM((ne, reach * nbr, width), F32),
             pltpu.VMEM((ne, reach * nbr, width), F32),
             pltpu.VMEM((2, order, order, pad, LANES), F32),
@@ -430,7 +459,7 @@
             pltpu.VMEM((2, packed * pad, LANES), F32),
             pltpu.VMEM((2 * reach, nbr, atoms), F32),
             dma((6,)), dma((2,)), dma((2,)), dma((reach,)), dma((reach,)),
-            dma((2 * reach, tiles)), dma((2 * reach, tiles)), dma((ne,)), dma((ne,)),
+            dma((2 * reach, parts)), dma((2 * reach, parts)), dma((ne,)), dma((ne,)),
         ],
         compiler_params=pltpu.CompilerParams(
             collective_id=0, has_side_effects=True, vmem_limit_bytes=67043328

time: 19.8 us -> 19.1 us (0.965)
  Pallas kernels: 19 us -> 18.3 us
    pallas_call x1, Pallas kernels: 16.7 us -> 16 us  [body(): pl.pallas_call(functools.partial(kernel, reach), out_shape=(jax.ShapeDtyp...]
where the time goes in v4:
time: 19.1 us; the launch traced here: 18.9 us
  Pallas kernels  18.3 us (96%)
  between operations  0.64 us (3%)
    pallas_call x1, Pallas kernels, body(): pl.pallas_call(functools.partial(kernel, reach), out_shape=(jax.ShapeDtyp...  16 us
    pallas_call x1, Pallas kernels, body(): pl.pallas_call(functools.partial(finish, reach), out_shape=(jax.ShapeDtyp...  2.32 us

profile of v4, /device:TPU:0, one launch (start us, length us, event | category | flops | bytes accessed | tf_op | source)
XLA Modules:
  0.0 18.9 jit_solution(7824737903415496527)
XLA Ops:
  0.6 16.0 %shard_map.86 = (bf16[80,384]{1,0:T(8,128)(2,1)}, f32[8,128]{1,0:T(8,128)}) custom-call(s32[48]{0:T(128)} %shift_ref.1, bf16[12,12,384]{2,1,0:T(8,128)(2,1)} %bitcast.4, bf16[144,4,384]{2,1,0:T(4,128)(2,1)} %bitcast.7, f32[96,4,384]{2,1,0:T(4,128)} %bitcast.6, s32[4,384]{1,0:T(4,128)} %near_hbm.1, bf16[144,80]{1,0:T(8,128)(2,1)} %constant.4.clone.e12_hbm), custom_call_target="tpu_custom_call" | custom-call | tf_op jit(solution)/shard_map/pallas_call | solution.py:432
  16.6 2.3 %shard_map.87 = (bf16[12,12,384]{2,1,0:T(8,128)(2,1)}, f32[48,4,48]{2,1,0:T(4,128)}) custom-call(s32[48]{0:T(128)} %shift_ref.1, bf16[12,12,384]{2,1,0:T(8,128)(2,1)} %bitcast.5, bf16[80,384]{1,0:T(8,128)(2,1)} %get-tuple-element.6.sig_ref, f32[8,128]{1,0:T(8,128)} %get-tuple-element.7.sum_ref, bf16[192,80]{1,0:T(8,128)(2,1)} %constant.5.clone.e16_ref), custom_call_target="tpu_custom_call" | custom-call | tf_op jit(solution)/shard_map/pallas_call | solution.py:475

commit v5 on v4

--- a/solution.py
+++ b/solution.py
@@ -44,7 +44,7 @@
     reach, shift_hbm, green_hbm, coup_hbm, weight_hbm, near_hbm, e12_hbm,
     sig_ref, sum_ref,
     shift_ref, green_ref, coup_ref, weight_ref, near_ref, e12_ref, tri32, own, halo, gin, pout, pin, pacc, hots, chunks, cin, c4, g3, pscr, ab,
-    load_sem, halo_send, halo_recv, gin_send, gin_recv, part_send, part_recv,
+    load_sem, hop_sem, halo_send, halo_recv, gin_send, gin_recv, part_send, part_recv,
     chunk_send, chunk_recv,
 ):
     order = green_ref.shape[0]
@@ -76,11 +76,36 @@
     load_shift = load(5, shift_hbm, shift_ref)
 
     barrier = pltpu.get_barrier_semaphore()
-    for r in range(1, ne):
+
+    def greet(sem, energy, row):
         pl.semaphore_signal(
-            barrier, inc=1, device_id={"energy": lax.rem(me + r, ne), "layer": layer},
-            device_id_type=MESH,
-        )
+            sem, inc=1, device_id={"energy": energy, "layer": row}, device_id_type=MESH
+        )
+
+    def greet_near(sem):
+        for d in range(1, reach + 1):
+
+            @pl.when(me + d < ne)
+            def _():
+                greet(sem, me + d, layer)
+
+            @pl.when(me >= d)
+            def _():
+                greet(sem, me - d, layer)
+
+    near_count = jnp.minimum(me, reach) + jnp.minimum(ne - 1 - me, reach)
+    rounds = -(-(ne - 1) // reach) - 1
+    passed = []
+
+    def pass_on():
+        n = len(passed)
+        if n < rounds:
+            pl.semaphore_wait(hop_sem.at[n], near_count)
+            if n + 1 < rounds:
+                greet_near(hop_sem.at[n + 1])
+            passed.append(n)
+
+    greet_near(barrier)
 
     @pl.when(layer > 0)
     def _():
@@ -120,7 +145,7 @@
             pin[2 * d - 1] = jnp.zeros(pin.shape[1:], BF16)
 
     pl.semaphore_wait(
-        barrier, ne - 1 + (layer > 0).astype(jnp.int32) + (layer < nl - 1).astype(jnp.int32)
+        barrier, near_count + (layer > 0).astype(jnp.int32) + (layer < nl - 1).astype(jnp.int32)
     )
 
     def remote(src, dst, send, recv, energy, row):
@@ -167,6 +192,9 @@
         @pl.when(me + d < ne)
         def _():
             green_copy(d).start()
+
+    if rounds:
+        greet_near(hop_sem.at[0])
 
     row = lax.broadcasted_iota(jnp.int32, (atoms, atoms), 0)
 
@@ -286,6 +314,8 @@
 
     correlate(0, 0, packed)
 
+    pass_on()
+
     @pl.when(has_below)
     def _():
         halo_copy(0).wait_recv()
@@ -300,8 +330,12 @@
 
     for n, (start, stop, first, final) in enumerate(plan):
         products(1, first, final)
+        if n == 0:
+            pass_on()
         correlate(1, start, stop)
         if stop == packed:
+            while len(passed) < rounds:
+                pass_on()
             corr = jnp.concatenate([jnp.concatenate(r, axis=1) for r in rows], axis=0)
             for e in range(ne):
                 moved = corr if e == 0 else pltpu.roll(corr, atoms - e * share, 1)
@@ -458,7 +492,8 @@
             pltpu.VMEM((order * order * pad, LANES), F32),
             pltpu.VMEM((2, packed * pad, LANES), F32),
             pltpu.VMEM((2 * reach, nbr, atoms), F32),
-            dma((6,)), dma((2,)), dma((2,)), dma((reach,)), dma((reach,)),
+            dma((6,)), pltpu.SemaphoreType.REGULAR((max(-(-(ne - 1) // reach) - 1, 1),)),
+            dma((2,)), dma((2,)), dma((reach,)), dma((reach,)),
             dma((2 * reach, parts)), dma((2 * reach, parts)), dma((ne,)), dma((ne,)),
         ],
         compiler_params=pltpu.CompilerParams(

time: 19.1 us -> 19.4 us (1.016)
  Pallas kernels: 18.3 us -> 18.6 us
    pallas_call x1, Pallas kernels: 16 us -> 16.3 us  [body(): pl.pallas_call(functools.partial(kernel, reach), out_shape=(jax.ShapeDtyp...]
where the time goes in v5:
time: 19.4 us; the launch traced here: 19.2 us
  Pallas kernels  18.6 us (96%)
  between operations  0.64 us (3%)
    pallas_call x1, Pallas kernels, body(): pl.pallas_call(functools.partial(kernel, reach), out_shape=(jax.ShapeDtyp...  16.3 us
    pallas_call x1, Pallas kernels, body(): pl.pallas_call(functools.partial(finish, reach), out_shape=(jax.ShapeDtyp...  2.32 us

profile of v5, /device:TPU:0, one launch (start us, length us, event | category | flops | bytes accessed | tf_op | source)
XLA Modules:
  0.0 19.2 jit_solution(12310754336520776793)
XLA Ops:
  0.6 16.3 %shard_map.86 = (bf16[80,384]{1,0:T(8,128)(2,1)}, f32[8,128]{1,0:T(8,128)}) custom-call(s32[48]{0:T(128)} %shift_ref.1, bf16[12,12,384]{2,1,0:T(8,128)(2,1)} %bitcast.4, bf16[144,4,384]{2,1,0:T(4,128)(2,1)} %bitcast.7, f32[96,4,384]{2,1,0:T(4,128)} %bitcast.6, s32[4,384]{1,0:T(4,128)} %near_hbm.1, bf16[144,80]{1,0:T(8,128)(2,1)} %constant.4.clone.e12_hbm), custom_call_target="tpu_custom_call" | custom-call | tf_op jit(solution)/shard_map/pallas_call | solution.py:466
  16.9 2.3 %shard_map.87 = (bf16[12,12,384]{2,1,0:T(8,128)(2,1)}, f32[48,4,48]{2,1,0:T(4,128)}) custom-call(s32[48]{0:T(128)} %shift_ref.1, bf16[12,12,384]{2,1,0:T(8,128)(2,1)} %bitcast.5, bf16[80,384]{1,0:T(8,128)(2,1)} %get-tuple-element.6.sig_ref, f32[8,128]{1,0:T(8,128)} %get-tuple-element.7.sum_ref, bf16[192,80]{1,0:T(8,128)(2,1)} %constant.5.clone.e16_ref), custom_call_target="tpu_custom_call" | custom-call | tf_op jit(solution)/shard_map/pallas_call | solution.py:510

commit v6 on v5

--- a/solution.py
+++ b/solution.py
@@ -42,8 +42,9 @@
 
 def kernel(
     reach, shift_hbm, green_hbm, coup_hbm, weight_hbm, near_hbm, e12_hbm,
-    sig_ref, sum_ref,
-    shift_ref, green_ref, coup_ref, weight_ref, near_ref, e12_ref, tri32, own, halo, gin, pout, pin, pacc, hots, chunks, cin, c4, g3, pscr, ab,
+    e16_hbm, cor_ref, sum_ref,
+    shift_ref, green_ref, coup_ref, weight_ref, near_ref, e12_ref, e16_ref, sig_ref,
+    g16, s16, l16, tri32, own, halo, gin, pout, pin, pacc, hots, chunks, cin, c4, g3, pscr, ab,
     load_sem, hop_sem, halo_send, halo_recv, gin_send, gin_recv, part_send, part_recv,
     chunk_send, chunk_recv,
 ):
@@ -74,6 +75,7 @@
     load_coup = load(3, coup_hbm, coup_ref)
     load_weight = load(4, weight_hbm, weight_ref)
     load_shift = load(5, shift_hbm, shift_ref)
+    load_e16 = load(6, e16_hbm, e16_ref)
 
     barrier = pltpu.get_barrier_semaphore()
 
@@ -315,6 +317,10 @@
     correlate(0, 0, packed)
 
     pass_on()
+    load_e16.wait()
+    g16[...] = jnp.zeros_like(g16)
+    for p in range(order):
+        g16[p, :order, :] = green_ref[p].astype(F32)
 
     @pl.when(has_below)
     def _():
@@ -373,51 +379,9 @@
             sigma = sigma + pin[s, start:stop].astype(F32)
         sig_ref[start:stop, :] = sigma.astype(BF16)
 
-    for r in range(1, ne):
-        chunk_copy(r).wait_recv()
-    summed = chunks[me]
-    for r in range(1, ne):
-        summed = summed + cin[r]
-    sum_ref[...] = summed * (1.0 / (order * math.sqrt(ne)))
-
-    @pl.when(has_above)
-    def _():
-        halo_copy(0).wait_send()
-
-    @pl.when(has_below)
-    def _():
-        halo_copy(1).wait_send()
-
-    for d in range(1, reach + 1):
-
-        @pl.when(me + d < ne)
-        def _():
-            green_copy(d).wait_send()
-            for n in range(len(plan)):
-                part_copy(2 * d - 2, n, me).wait_send()
-
-        @pl.when(me >= d)
-        def _():
-            for n in range(len(plan)):
-                part_copy(2 * d - 1, n, me).wait_send()
-
-    for r in range(1, ne):
-        chunk_copy(r).wait_send()
-
-
-def finish(
-    reach, shift_ref, green_ref, sig_ref, sum_ref, e16_ref, out_ref, pol_ref, g16, s16, l16
-):
-    order = green_ref.shape[0]
-    nbr, share = pol_ref.shape[1:]
-    freqs = shift_ref.shape[0]
-    rows = g16.shape[1]
     s16[...] = jnp.dot(
         e16_ref[...], sig_ref[...], preferred_element_type=F32
     ).reshape(s16.shape)
-    g16[...] = jnp.zeros_like(g16)
-    for p in range(order):
-        g16[p, :order, :] = green_ref[p].astype(F32)
 
     for i in range(0, order, 2):
         left = [g16[i + n, 0:1, :] * s16[0] for n in range(2)]
@@ -432,8 +396,44 @@
             block = g16[p]
             total = [total[n] + l16[i + n, p : p + 1, :] * block for n in range(2)]
         for n in range(2):
-            out_ref[i + n] = total[n][:order].astype(BF16)
-
+            cor_ref[i + n] = total[n][:order].astype(BF16)
+
+    for r in range(1, ne):
+        chunk_copy(r).wait_recv()
+    summed = chunks[me]
+    for r in range(1, ne):
+        summed = summed + cin[r]
+    sum_ref[...] = summed * (1.0 / (order * math.sqrt(ne)))
+
+    @pl.when(has_above)
+    def _():
+        halo_copy(0).wait_send()
+
+    @pl.when(has_below)
+    def _():
+        halo_copy(1).wait_send()
+
+    for d in range(1, reach + 1):
+
+        @pl.when(me + d < ne)
+        def _():
+            green_copy(d).wait_send()
+            for n in range(len(plan)):
+                part_copy(2 * d - 2, n, me).wait_send()
+
+        @pl.when(me >= d)
+        def _():
+            for n in range(len(plan)):
+                part_copy(2 * d - 1, n, me).wait_send()
+
+    for r in range(1, ne):
+        chunk_copy(r).wait_send()
+
+
+def finish(reach, shift_ref, cor_ref, sum_ref, out_ref, pol_ref):
+    nbr, share = pol_ref.shape[1:]
+    freqs = shift_ref.shape[0]
+    out_ref[...] = cor_ref[...]
     summed = sum_ref[:, :share]
     for w in range(freqs):
         shift = shift_ref[w]
@@ -463,13 +463,13 @@
     hbm = pl.BlockSpec(memory_space=pltpu.HBM)
     dma = pltpu.SemaphoreType.DMA
     green = green_blocks[0]
-    sigma, summed = pl.pallas_call(
+    result, summed = pl.pallas_call(
         functools.partial(kernel, reach),
         out_shape=(
-            jax.ShapeDtypeStruct((packed, atoms), BF16),
+            jax.ShapeDtypeStruct((order, order, atoms), BF16),
             jax.ShapeDtypeStruct((reach * nbr, width), F32),
         ),
-        in_specs=[hbm] * 6,
+        in_specs=[hbm] * 7,
         out_specs=(vmem, vmem),
         scratch_shapes=[
             pltpu.SMEM((freqs,), jnp.int32),
@@ -478,6 +478,11 @@
             pltpu.VMEM((2 * freqs, nbr, atoms), F32),
             pltpu.VMEM((nbr, atoms), jnp.int32),
             pltpu.VMEM((order * order, packed), BF16),
+            pltpu.VMEM((order * rows, packed), BF16),
+            pltpu.VMEM((packed, atoms), BF16),
+            pltpu.VMEM((order, rows, atoms), F32),
+            pltpu.VMEM((order, rows, atoms), F32),
+            pltpu.VMEM((order, rows, atoms), F32),
             pltpu.VMEM((packed, atoms), F32),
             pltpu.VMEM((packed, atoms), BF16),
             pltpu.VMEM((2, packed, atoms), BF16),
@@ -492,7 +497,7 @@
             pltpu.VMEM((order * order * pad, LANES), F32),
             pltpu.VMEM((2, packed * pad, LANES), F32),
             pltpu.VMEM((2 * reach, nbr, atoms), F32),
-            dma((6,)), pltpu.SemaphoreType.REGULAR((max(-(-(ne - 1) // reach) - 1, 1),)),
+            dma((7,)), pltpu.SemaphoreType.REGULAR((max(-(-(ne - 1) // reach) - 1, 1),)),
             dma((2,)), dma((2,)), dma((reach,)), dma((reach,)),
             dma((2 * reach, parts)), dma((2 * reach, parts)), dma((ne,)), dma((ne,)),
         ],
@@ -506,6 +511,7 @@
         phonon_weights.reshape(2 * freqs, nbr, atoms),
         neighbours,
         expansion(order, order, packed),
+        expansion(order, rows, packed),
     )
     corrected, polarization = pl.pallas_call(
         functools.partial(finish, reach),
@@ -513,11 +519,10 @@
             jax.ShapeDtypeStruct((order, order, atoms), BF16),
             jax.ShapeDtypeStruct((freqs, nbr, share), F32),
         ),
-        in_specs=[smem, vmem, vmem, vmem, vmem],
+        in_specs=[smem, vmem, vmem],
         out_specs=(vmem, vmem),
-        scratch_shapes=[pltpu.VMEM((order, rows, atoms), F32)] * 3,
         compiler_params=pltpu.CompilerParams(vmem_limit_bytes=67043328),
-    )(phonon_shifts, green, sigma, summed, expansion(order, rows, packed))
+    )(phonon_shifts, result, summed)
     return corrected[None], polarization
 
 

time: 19.4 us -> 18.8 us (0.969)
  Pallas kernels: 18.6 us -> 18 us
    pallas_call x1, Pallas kernels: 2.32 us -> 1.72 us  [body(): pl.pallas_call(functools.partial(finish, reach), out_shape=(jax.ShapeDtyp...]
where the time goes in v6:
time: 18.8 us; the launch traced here: 18.7 us
  Pallas kernels  18 us (96%)
  between operations  0.64 us (3%)
    pallas_call x1, Pallas kernels, body(): pl.pallas_call(functools.partial(kernel, reach), out_shape=(jax.ShapeDtyp...  16.3 us
    pallas_call x1, Pallas kernels, body(): pl.pallas_call(functools.partial(finish, reach), out_shape=(jax.ShapeDtyp...  1.72 us

profile of v6, /device:TPU:0, one launch (start us, length us, event | category | flops | bytes accessed | tf_op | source)
XLA Modules:
  0.0 18.7 jit_solution(15882360265853547462)
XLA Ops:
  0.6 16.3 %shard_map.86 = (bf16[12,12,384]{2,1,0:T(8,128)(2,1)}, f32[8,128]{1,0:T(8,128)}) custom-call(s32[48]{0:T(128)} %shift_ref.1, bf16[12,12,384]{2,1,0:T(8,128)(2,1)} %bitcast.6, bf16[144,4,384]{2,1,0:T(4,128)(2,1)} %bitcast.5, f32[96,4,384]{2,1,0:T(4,128)} %bitcast.4, s32[4,384]{1,0:T(4,128)} %near_hbm.1, bf16[144,80]{1,0:T(8,128)(2,1)} %constant.4.clone.e12_hbm, ...), custom_call_target="tpu_custom_call" | custom-call | tf_op jit(solution)/shard_map/pallas_call | solution.py:466
  17.0 1.7 %shard_map.87 = (bf16[12,12,384]{2,1,0:T(8,128)(2,1)}, f32[48,4,48]{2,1,0:T(4,128)}) custom-call(s32[48]{0:T(128)} %shift_ref.1, bf16[12,12,384]{2,1,0:T(8,128)(2,1)} %get-tuple-element.6.cor_ref, f32[8,128]{1,0:T(8,128)} %get-tuple-element.7.sum_ref), custom_call_target="tpu_custom_call" | custom-call | tf_op jit(solution)/shard_map/pallas_call | solution.py:516
